TPU v7x, 128 devices: a whole 4x4x4 slice. The times are simulated.
128 devices in a mesh: section: 4 (over x), dev: 32 (over y, z, core).
Axes of the slice: x: 4, y: 4, z: 4, core: 2. Of those that a mesh axis runs over, the one named last changes fastest.
Arguments:
- hidden: bfloat16 [1024, 2048], P('dev'), may hold values from -8 to 8
- lengths: int32 [1024], P('dev'), may hold values from 1 to 256, as said below
- attn_gain: float32 [2048], replicated, may hold values from 0.1 to 1.9
- w_query: bfloat16 [2048, 3072], P(None, 'section'), may hold values from -0.125 to 0.125
- w_latent: bfloat16 [2048, 512], replicated, may hold values from -0.125 to 0.125
- latent_gain: float32 [512], replicated, may hold values from 0.1 to 1.9
- w_rope_key: bfloat16 [64, 2048], replicated, may hold values from -0.125 to 0.125
- w_key_up: bfloat16 [16, 512, 128], P('section'), may hold values from -0.5 to 0.5
- w_value_up: bfloat16 [16, 512, 128], P('section'), may hold values from -0.25 to 0.25
- w_out: bfloat16 [2048, 2048], P('section'), may hold values from -0.125 to 0.125
- latent_cache: bfloat16 [1024, 256, 512], P('dev'), may hold values from -6 to 6
- rope_cache: bfloat16 [1024, 64, 256], P('dev'), may hold values from -1200 to 1200
- ffn_gain: float32 [2048], replicated, may hold values from 0.1 to 1.9
- expert_ids: int32 [1024, 6], P('dev'), may hold values from 0 to 63, all different within a row; in each aligned block of 8 rows (0 to 7, 8 to 15, ...) at most 2 rows name the same one
- route_weights: float32 [1024, 6], P('dev'), may hold values from 0.05 to 0.5
- w_gate_up: bfloat16 [64, 2, 1408, 2048], P('dev', None, 'section'), may hold values from -0.125 to 0.125
- w_down: bfloat16 [64, 1408, 2048], P('dev', 'section'), may hold values from -0.15625 to 0.15625
Outputs:
- layer_out: bfloat16 [1024, 2048], P('dev')
Inputs may be any that keep to these rules, and one draw needn't show every extreme that they name: `lengths`: every aligned block of 32 rows holds a row of length 256. `expert_ids`: each row names 6 different experts. In every aligned block of 8 rows no expert is named by more than 2 rows, and some block has an expert named by exactly 2.
All inputs are finite; a program needn't handle non-finite values.
Results may differ from a plain program's by a relative error of at most 0.011.
Values may be sent and summed in bfloat16 or wider, within the bound.
No kernel may reach another device: no remote copies, remote signals or barrier semaphores. Data moves between devices by JAX's collectives and lax.ppermute only.
A program may use at most 128 MiB of HBM per device.

v0:
```python
import jax
import jax.numpy as jnp
from jax import lax
from jax.sharding import PartitionSpec as P

EXPERTS = 64
MOST = 2


epsilon = 1e-06
far_below = -1e30


def rms_norm(values, norm_gain):
    mean_square = jnp.mean(values * values, axis=-1, keepdims=True)
    return values * lax.rsqrt(mean_square + epsilon) * norm_gain


def rotary(values, positions):
    half_width = values.shape[-1] // 2
    step_index = jnp.arange(half_width, dtype=jnp.float32)
    frequency = jnp.exp(-jnp.log(10000.0) * step_index / half_width)
    angles = positions.astype(jnp.float32)[:, None] * frequency[None, :]
    if values.ndim == 3:
        angles = angles[:, None, :]
    cosine = jnp.cos(angles)
    sine_part = jnp.sin(angles)
    first_half = values[..., :half_width]
    second = values[..., half_width:]
    return jnp.concatenate(
        [first_half * cosine - second * sine_part, second * cosine + first_half * sine_part],
        axis=-1,
    )


def slot_targets(expert_ids, block_rows):
    row_count, top_count = expert_ids.shape
    blocks = row_count // block_rows
    flat_ids = expert_ids.reshape(blocks, block_rows * top_count)
    onehot = (flat_ids[:, :, None] == jnp.arange(EXPERTS, dtype=jnp.int32)[None, None, :]).astype(
        jnp.int32
    )
    earlier = jnp.cumsum(onehot, axis=1) - onehot
    rank_in = jnp.sum(earlier * onehot, axis=2)
    capacity = blocks * MOST
    target = flat_ids * capacity + jnp.arange(blocks, dtype=jnp.int32)[:, None] * MOST + rank_in
    return (target.reshape(row_count, top_count), capacity)


def pack_rows(source, target, capacity):
    slot_count = EXPERTS * capacity
    hit_table = (
        target[:, :, None] == jnp.arange(slot_count, dtype=jnp.int32)[None, None, :]
    ).astype(jnp.bfloat16)
    hit_table = jnp.sum(hit_table, axis=1)
    packed = lax.dot_general(
        hit_table, source, (((0,), (0,)), ((), ())), preferred_element_type=jnp.float32
    )
    return packed.astype(jnp.bfloat16)


def expert_part(slot_rows, w_gate_up, w_down):
    gate_up = jnp.einsum(
        "secx,egfx->secgf", slot_rows, w_gate_up, preferred_element_type=jnp.float32
    )
    activated = (jax.nn.silu(gate_up[:, :, :, 0, :]) * gate_up[:, :, :, 1, :]).astype(jnp.bfloat16)
    return jnp.einsum("secf,efx->secx", activated, w_down, preferred_element_type=jnp.float32)


def combine_rows(middle, expert_out, target, route_weights):
    flat_out = expert_out.reshape(-1, expert_out.shape[-1])
    routed = jnp.take(flat_out, target.reshape(-1), axis=0)
    routed = routed.reshape(target.shape + (flat_out.shape[1],)).astype(jnp.float32)
    layer_out = middle.astype(jnp.float32) + jnp.sum(route_weights[:, :, None] * routed, axis=1)
    return layer_out.astype(jnp.bfloat16)


def attend(
    query_latent, query_rope, latent_new, key_new, latent_cache, rope_cache, lengths, score_scale
):
    scores = jnp.einsum(
        "rhl,rtl->rht", query_latent, latent_cache, preferred_element_type=jnp.float32
    )
    scores = scores + jnp.einsum(
        "rhp,rpt->rht", query_rope, rope_cache, preferred_element_type=jnp.float32
    )
    scores = scores * score_scale
    self_score = jnp.einsum(
        "rhl,rl->rh", query_latent, latent_new, preferred_element_type=jnp.float32
    )
    self_score = (
        self_score
        + jnp.einsum("rhp,rp->rh", query_rope, key_new, preferred_element_type=jnp.float32)
    ) * score_scale
    places = jnp.arange(latent_cache.shape[1], dtype=jnp.int32)
    valid_mask = places[None, None, :] < lengths[:, None, None]
    masked = jnp.where(valid_mask, scores, far_below)
    peak_score = jnp.maximum(jnp.max(masked, axis=2), self_score)
    weights = jnp.where(valid_mask, jnp.exp(masked - peak_score[:, :, None]), 0.0)
    self_weight = jnp.exp(self_score - peak_score)
    totals = jnp.sum(weights, axis=2) + self_weight
    prob_cache = (weights / totals[:, :, None]).astype(jnp.bfloat16)
    prob_self = (self_weight / totals).astype(jnp.bfloat16)
    mixed = jnp.einsum("rht,rtl->rhl", prob_cache, latent_cache, preferred_element_type=jnp.float32)
    mixed = (
        mixed
        + prob_self.astype(jnp.float32)[:, :, None] * latent_new.astype(jnp.float32)[:, None, :]
    )
    return mixed.astype(jnp.bfloat16)


def per_device(
    hidden,
    lengths,
    attn_gain,
    w_query,
    w_latent,
    latent_gain,
    w_rope_key,
    w_key_up,
    w_value_up,
    w_out,
    latent_cache,
    rope_cache,
    ffn_gain,
    expert_ids,
    route_weights,
    w_gate_up,
    w_down,
):
    sections = lax.axis_size("section")
    devices = lax.axis_size("dev")
    row_count = hidden.shape[0]
    quarter = row_count // sections
    model_width = hidden.shape[1]
    head_local = w_key_up.shape[0]
    nope_width = w_key_up.shape[2]
    rope_width = w_rope_key.shape[0]
    score_scale = (nope_width + rope_width) ** (-0.5)
    normed = rms_norm(hidden.astype(jnp.float32), attn_gain).astype(jnp.bfloat16)
    queries = jnp.dot(normed, w_query, preferred_element_type=jnp.float32).astype(jnp.bfloat16)
    queries = queries.reshape(row_count, head_local, nope_width + rope_width)
    query_rope = rotary(queries[:, :, nope_width:].astype(jnp.float32), lengths).astype(
        jnp.bfloat16
    )
    query_latent = jnp.einsum(
        "rhn,hln->rhl", queries[:, :, :nope_width], w_key_up, preferred_element_type=jnp.float32
    ).astype(jnp.bfloat16)
    latent_new = rms_norm(
        jnp.dot(normed, w_latent, preferred_element_type=jnp.float32), latent_gain
    ).astype(jnp.bfloat16)
    key_raw = lax.dot_general(
        normed, w_rope_key, (((1,), (1,)), ((), ())), preferred_element_type=jnp.float32
    )
    key_new = rotary(key_raw, lengths).astype(jnp.bfloat16)
    mixed_latent = attend(
        query_latent,
        query_rope,
        latent_new,
        key_new,
        latent_cache,
        rope_cache,
        lengths,
        score_scale,
    )
    head_out = jnp.einsum(
        "rhl,hlv->rhv", mixed_latent, w_value_up, preferred_element_type=jnp.float32
    ).astype(jnp.bfloat16)
    heads_flat = head_out.reshape(row_count, -1)
    partial_value = jnp.dot(heads_flat, w_out, preferred_element_type=jnp.float32)
    attention = lax.psum(partial_value, "section")
    middle = (hidden.astype(jnp.float32) + attention).astype(jnp.bfloat16)
    expert_in = rms_norm(middle.astype(jnp.float32), ffn_gain).astype(jnp.bfloat16)
    target, capacity = slot_targets(expert_ids, quarter)
    packed = pack_rows(expert_in, target, capacity).reshape(devices, -1, capacity, model_width)
    partial_out = expert_part(
        lax.all_to_all(packed, "dev", split_axis=0, concat_axis=0, tiled=True), w_gate_up, w_down
    )
    returned = lax.all_to_all(
        partial_out.astype(jnp.bfloat16), "dev", split_axis=0, concat_axis=0, tiled=True
    ).astype(partial_out.dtype)
    expert_out = lax.psum(returned.astype(jnp.bfloat16), "section")
    return combine_rows(middle, expert_out, target, route_weights)


def solution(mesh):
    in_specs = (
        P("dev", None),
        P("dev"),
        P(),
        P(None, "section"),
        P(),
        P(),
        P(),
        P("section", None, None),
        P("section", None, None),
        P("section", None),
        P("dev", None, None),
        P("dev", None, None),
        P(),
        P("dev", None),
        P("dev", None),
        P("dev", None, "section", None),
        P("dev", "section", None),
    )
    out_specs = P("dev", None)
    return jax.shard_map(
        per_device, mesh=mesh, in_specs=in_specs, out_specs=out_specs, check_vma=False
    )
```

profile of v0, /device:TPU:1, one launch (start us, length us, event | category | flops | bytes accessed | tf_op | source)
XLA Modules:
  0.0 220.6 jit_solution(4492424188257684018)
XLA Ops:
  6.6 0.5 multiply_exponential_fusion
  7.1 1.3 fusion.22
  8.5 2.2 %convolution_convert_fusion.3 = bf16[32,768]{1,0:T(8,128)(2,1)} fusion(bf16[2048,768]{1,0:T(8,128)(2,1)S(1)} %copy-done, bf16[32,2048]{1,0:T(8,128)(2,1)} %param.17, f32[2048]{0:T(1024)} %param.19, f32[32]{0:T(128)S(1)} %add_rsqrt_fusion.2), kind=kOutput, calls=%fused_computation.17 | convolution fusion | flops 100950016 | bytes 3334272 | tf_op jit(solution)/shard_map/dot_general | solution.py:141
  10.7 1.5 reshape.195
  12.3 0.9 slice_convert_fusion
  13.6 0.9 subtract_convert_fusion.1
  14.9 1.5 fusion.56
  16.5 0.6 multiply_reduce_fusion.1
  17.8 5.9 %fusion.65 = (f32[32,4]{1,0:T(8,128)S(1)}, f32[32,4,256]{2,1,0:T(4,128)S(1)}) fusion(f32[32,4,256]{2,1,0:T(4,128)S(1)} %fusion.56, bf16[32,256,512]{2,1,0:T(8,128)(2,1)} %param.27, bf16[32,4,512]{2,0,1:T(8,128)(2,1)S(1)} %fusion.13, pred[32,256]{1,0:T(8,128)(4,1)S(1)} %iota_compare_fusion.2), kind=kOutput, calls=%fused_computation.101 | convolution fusion | flops 33685376 | bytes 8790528 | tf_op jit(solution)/shard_map/rhl,rtl->rht/dot_general | solution.py:81
  24.0 1.2 fusion.12
  25.7 1.2 fusion.45
  28.1 41.6 %all-reduce.3.cloned.1.call-done = f32[32,2048]{1,0:T(8,128)} async-done(((f32[32,2048]{1,0:T(8,128)}), f32[32,2048]{1,0:T(8,128)}) %all-reduce.3.cloned.1.call-update) | async-done | bytes 262160 | tf_op jit(solution)/shard_map/psum | solution.py:171
  69.7 1.1 fusion.26
  70.9 0.8 convolution_convert_fusion
  71.6 37.8 %all_to_all.10 = bf16[32,2,8,2048]{3,2,1,0:T(8,128)(2,1)S(1)} all-to-all(bf16[32,2,8,2048]{3,2,1,0:T(8,128)(2,1)S(1)} %bitcast.68), channel_id=1, replica_groups=mesh['section'=4,'dev'=32] {'dev'}, dimensions={0} | all-to-all | bytes 4194304 | tf_op jit(solution)/shard_map/all_to_all | solution.py:177
  109.4 4.8 %fusion.7 = f32[32,2,8,2,352]{4,2,3,0,1:T(8,128)S(1)} fusion(bf16[2,2,352,2048]{3,2,1,0:T(8,128)(2,1)} %param.32, bf16[32,2,8,2048]{3,2,1,0:T(8,128)(2,1)S(1)} %all_to_all.10), kind=kOutput, calls=%fused_computation.9 | convolution fusion | flops 1476395008 | bytes 9306112 | tf_op jit(solution)/shard_map/secx,egfx->secgf/dot_general | solution.py:63
  114.2 1.3 fusion.3
  115.8 32.0 %all_to_all.11 = bf16[32,2,8,2048]{3,2,1,0:T(8,128)(2,1)} all-to-all(bf16[32,2,8,2048]{3,2,1,0:T(8,128)(2,1)S(1)} %copy.56), channel_id=1, replica_groups=mesh['section'=4,'dev'=32] {'dev'}, dimensions={0} | all-to-all | bytes 4194304 | tf_op jit(solution)/shard_map/all_to_all | solution.py:179
  148.1 0.3 copy-done.10
  148.6 54.8 %all-reduce.5.cloned.1.call-done = bf16[512,2048]{1,0:T(8,128)(2,1)} async-done(((bf16[512,2048]{1,0:T(8,128)(2,1)}), bf16[512,2048]{1,0:T(8,128)(2,1)}) %all-reduce.5.cloned.1.call-update) | async-done | bytes 2097168 | tf_op jit(solution)/shard_map/psum | solution.py:182
  203.3 4.7 %gather_fusion = bf16[192,2048]{1,0:T(8,128)(2,1)} fusion(bf16[512,2048]{1,0:T(8,128)(2,1)} %all-reduce.5.cloned.1.call-done, s32[1024]{0:T(1024)S(1)} %pad_clamp_fusion), kind=kCustom, calls=%fused_computation | custom fusion | bytes 1573632 | tf_op jit(solution)/shard_map/jit(_take)/gather | solution.py:72
  208.0 2.2 gather.7
  210.2 2.9 %multiply_reduce_fusion = f32[32,2048]{1,0:T(8,128)S(1)} fusion(bf16[32,6,2048]{2,1,0:T(8,128)(2,1)} %gather.7, f32[32,6]{1,0:T(8,128)S(1)} %copy.50, pred[32,6]{1,0:T(8,128)(4,1)S(1)} %get-tuple-element.5), kind=kLoop, calls=%fused_computation.8 | loop fusion | flops 1507328 | bytes 1049536 | tf_op jit(solution)/shard_map/reduce_sum | solution.py:74
  213.1 0.7 fusion.29
  (75 shorter events, 4.1 us)
Async XLA Ops:
  6.5 2.0 copy-start
  6.5 6.8 %copy-start.1 = (bf16[32,2048]{1,0:T(8,128)(2,1)S(1)}, bf16[32,2048]{1,0:T(8,128)(2,1)}, u32[]{:S(2)}) copy-start(bf16[32,2048]{1,0:T(8,128)(2,1)} %param.17) | copy-start | bytes 393220
  6.5 6.8 %copy-start.7 = (f32[2048]{0:T(1024)S(1)}, f32[2048]{0:T(1024)}, u32[]{:S(2)}) copy-start(f32[2048]{0:T(1024)} %param.19) | copy-start | bytes 24580
  6.5 6.6 %copy-start.12 = (s32[32]{0:T(128)S(1)}, s32[32]{0:T(128)}, u32[]{:S(2)}) copy-start(s32[32]{0:T(128)} %param.18) | copy-start | bytes 388
  6.5 6.8 %copy-start.6 = (bf16[64,2048]{1,0:T(8,128)(2,1)S(1)}, bf16[64,2048]{1,0:T(8,128)(2,1)}, u32[]{:S(2)}) copy-start(bf16[64,2048]{1,0:T(8,128)(2,1)} %param.23) | copy-start | bytes 786436
  6.5 63.2 %all-reduce.3.cloned.1.call-start = ((), (), s32[]{:S(2)}) async-start(), calls=%async_computation.2 | async-start | bytes 524288 | tf_op jit(solution)/shard_map/psum | solution.py:171
  12.3 4.2 %copy-start.3 = (bf16[2048,512]{1,0:T(8,128)(2,1)S(1)}, bf16[2048,512]{1,0:T(8,128)(2,1)}, u32[]{:S(2)}) copy-start(bf16[2048,512]{1,0:T(8,128)(2,1)} %param.21) | copy-start | bytes 6291460
  12.3 5.2 %copy-start.11 = (f32[512]{0:T(512)S(1)}, f32[512]{0:T(512)}, u32[]{:S(2)}) copy-start(f32[512]{0:T(512)} %param.22) | copy-start | bytes 6148
  13.2 3.9 %copy-start.4 = (bf16[4,512,128]{2,1,0:T(8,128)(2,1)S(1)}, bf16[4,512,128]{2,1,0:T(8,128)(2,1)}, u32[]{:S(2)}) copy-start(bf16[4,512,128]{2,1,0:T(8,128)(2,1)} %param.24) | copy-start | bytes 1572868
  13.2 3.9 %slice-start.2 = ((bf16[32,4,192]{2,1,0:T(4,128)(2,1)}), bf16[32,4,128]{2,1,0:T(4,128)(2,1)S(1)}, s32[]{:S(2)}) async-start(bf16[32,4,192]{2,1,0:T(4,128)(2,1)} %reshape.195), calls=%async_computation.6 | async-start | bytes 65536 | tf_op jit(solution)/shard_map/slice | solution.py:147
  13.3 10.6 %slice-start = ((s8[8388608]{0:T(1024)(128)(4,1)}), s8[4194304]{0:T(1024)(128)(4,1)S(1)}, s32[]{:S(2)}) async-start(s8[8388608]{0:T(1024)(128)(4,1)} %bitcast.65), calls=%async_computation.4 | async-start | bytes 8388608
  17.8 6.2 %slice-start.1 = ((s8[8388608]{0:T(1024)(128)(4,1)}), s8[4194304]{0:T(1024)(128)(4,1)S(1)}, s32[]{:S(2)}) async-start(s8[8388608]{0:T(1024)(128)(4,1)} %bitcast.65), calls=%async_computation.5 | async-start | bytes 8388608
  23.9 1.3 copy-start.5
  24.0 1.8 copy-start.2
  25.2 1.8 copy-start.9
  25.2 45.6 %copy-start.8 = (f32[2048]{0:T(1024)S(1)}, f32[2048]{0:T(1024)}, u32[]{:S(2)}) copy-start(f32[2048]{0:T(1024)} %param.29) | copy-start | bytes 24580
  26.9 176.4 %all-reduce.5.cloned.1.call-start = ((), (), s32[]{:S(2)}) async-start(), calls=%async_computation.3 | async-start | bytes 4194304 | tf_op jit(solution)/shard_map/psum | solution.py:182
  109.4 4.8 %copy-start.13 = (bf16[2,352,2048]{2,1,0:T(8,128)(2,1)S(1)}, bf16[2,352,2048]{2,1,0:T(8,128)(2,1)}, u32[]{:S(2)}) copy-start(bf16[2,352,2048]{2,1,0:T(8,128)(2,1)} %param.33) | copy-start | bytes 8650756
  147.8 0.7 copy-start.10
Sparse Core Ops, SparseCore 0:
  27.0 42.6 all-reduce.2
  147.9 55.3 all-reduce.4
where the time goes:
time: 221 us
  waiting for transfers between devices  96.4 us (44%)
  blocking collectives  69.8 us (32%)
  matrix products  20.7 us (9%)
  between operations  13.7 us (6%)
  local copies, waits for them, and re-layouts  10.3 us (5%)
  other arithmetic  9.69 us (4%)
    psum x1, waiting for transfers between devices, per_device(): expert_out = lax.psum(returned.astype(jnp.bfloat16), 'section')  54.8 us
    psum x1, waiting for transfers between devices, per_device(): attention = lax.psum(partial_value, 'section')  41.6 us
    all_to_all x1, blocking collectives, per_device(): lax.all_to_all(packed, 'dev', split_axis=0, concat_axis=0, tiled=True)  37.8 us
    all_to_all x1, blocking collectives, per_device(): lax.all_to_all(partial_out.astype(jnp.bfloat16), 'dev', split_axis=0, con...  32 us
    gather x2, local copies, waits for them, and re-layouts, combine_rows(): routed = jnp.take(flat_out, target.reshape(-1), axis=0)  6.85 us
    dot_general x1, matrix products, attend(): jnp.einsum('rhl,rtl->rht', query_latent, latent_cache, preferred_element_...  5.89 us
    dot_general x1, matrix products, expert_part(): jnp.einsum('secx,egfx->secgf', slot_rows, w_gate_up, preferred_element_ty...  4.8 us
  transfers between devices with their start and end apart: 2, of which 2 were waited for; matrix products, arithmetic and copies ran while one was open for 1% of the time, Pallas kernels for 0%

commit v1 on v0

--- a/solution.py
+++ b/solution.py
@@ -5,6 +5,7 @@
 
 EXPERTS = 64
 MOST = 2
+ROW_Q = 8
 
 
 epsilon = 1e-06
@@ -36,14 +37,14 @@
 def slot_targets(expert_ids, block_rows):
     row_count, top_count = expert_ids.shape
     blocks = row_count // block_rows
-    flat_ids = expert_ids.reshape(blocks, block_rows * top_count)
-    onehot = (flat_ids[:, :, None] == jnp.arange(EXPERTS, dtype=jnp.int32)[None, None, :]).astype(
-        jnp.int32
-    )
-    earlier = jnp.cumsum(onehot, axis=1) - onehot
-    rank_in = jnp.sum(earlier * onehot, axis=2)
+    ids = expert_ids.reshape(blocks, block_rows, top_count)
+    same = ids[:, :, :, None, None] == ids[:, None, None, :, :]
+    row_index = jnp.arange(block_rows, dtype=jnp.int32)
+    earlier = row_index[:, None, None, None] > row_index[None, None, :, None]
+    rank_in = jnp.sum((same & earlier[None]).astype(jnp.int32), axis=(3, 4))
     capacity = blocks * MOST
-    target = flat_ids * capacity + jnp.arange(blocks, dtype=jnp.int32)[:, None] * MOST + rank_in
+    block_index = jnp.arange(blocks, dtype=jnp.int32)[:, None, None]
+    target = ids * capacity + block_index * MOST + rank_in
     return (target.reshape(row_count, top_count), capacity)
 
 
@@ -67,12 +68,27 @@
     return jnp.einsum("secf,efx->secx", activated, w_down, preferred_element_type=jnp.float32)
 
 
-def combine_rows(middle, expert_out, target, route_weights):
-    flat_out = expert_out.reshape(-1, expert_out.shape[-1])
-    routed = jnp.take(flat_out, target.reshape(-1), axis=0)
-    routed = routed.reshape(target.shape + (flat_out.shape[1],)).astype(jnp.float32)
-    layer_out = middle.astype(jnp.float32) + jnp.sum(route_weights[:, :, None] * routed, axis=1)
-    return layer_out.astype(jnp.bfloat16)
+def section_sum(partial):
+    sections = lax.axis_size("section")
+    shifted = [
+        lax.ppermute(partial, "section", [(i, (i + step) % sections) for i in range(sections)])
+        for step in range(1, sections)
+    ]
+    held = [value.astype(jnp.float32) for value in [partial] + shifted]
+    half = sections // 2
+    pairs = [held[i] + held[i + half] for i in range(half)]
+    return sum(pairs[1:], pairs[0])
+
+
+def combine_rows(returned, target, route_weights):
+    flat_out = returned.reshape(-1, returned.shape[-1])
+    slots = jnp.arange(flat_out.shape[0], dtype=jnp.int32)
+    hits = target[:, :, None] == slots[None, None, :]
+    table = jnp.sum(jnp.where(hits, route_weights[:, :, None], 0.0), axis=1)
+    upper = lax.reduce_precision(table, 8, 7)
+    both = jnp.concatenate([upper, table - upper], axis=0).astype(jnp.bfloat16)
+    sums = jnp.dot(both, flat_out, preferred_element_type=jnp.float32)
+    return sums[: target.shape[0]] + sums[target.shape[0] :]
 
 
 def attend(
@@ -128,10 +144,9 @@
     w_gate_up,
     w_down,
 ):
-    sections = lax.axis_size("section")
     devices = lax.axis_size("dev")
     row_count = hidden.shape[0]
-    quarter = row_count // sections
+    block_rows = ROW_Q
     model_width = hidden.shape[1]
     head_local = w_key_up.shape[0]
     nope_width = w_key_up.shape[2]
@@ -168,19 +183,19 @@
     ).astype(jnp.bfloat16)
     heads_flat = head_out.reshape(row_count, -1)
     partial_value = jnp.dot(heads_flat, w_out, preferred_element_type=jnp.float32)
-    attention = lax.psum(partial_value, "section")
+    attention = section_sum(partial_value.astype(jnp.bfloat16))
     middle = (hidden.astype(jnp.float32) + attention).astype(jnp.bfloat16)
     expert_in = rms_norm(middle.astype(jnp.float32), ffn_gain).astype(jnp.bfloat16)
-    target, capacity = slot_targets(expert_ids, quarter)
+    target, capacity = slot_targets(expert_ids, block_rows)
     packed = pack_rows(expert_in, target, capacity).reshape(devices, -1, capacity, model_width)
     partial_out = expert_part(
         lax.all_to_all(packed, "dev", split_axis=0, concat_axis=0, tiled=True), w_gate_up, w_down
     )
     returned = lax.all_to_all(
         partial_out.astype(jnp.bfloat16), "dev", split_axis=0, concat_axis=0, tiled=True
-    ).astype(partial_out.dtype)
-    expert_out = lax.psum(returned.astype(jnp.bfloat16), "section")
-    return combine_rows(middle, expert_out, target, route_weights)
+    )
+    routed = section_sum(combine_rows(returned, target, route_weights).astype(jnp.bfloat16))
+    return (middle.astype(jnp.float32) + routed).astype(jnp.bfloat16)
 
 
 def solution(mesh):

time: 221 us -> 125 us (0.57)
  waiting for transfers between devices: 96.4 us -> 34.8 us
  blocking collectives: 69.8 us -> 37.6 us
  starting transfers between devices: 0.08 us -> 13.8 us
  between operations: 13.7 us -> 0.36 us
  local copies, waits for them, and re-layouts: 10.3 us -> 5.6 us
    psum x2 -> x0, waiting for transfers between devices: 96.4 us -> none  [the longest x1 54.8 us: per_device(): expert_out = lax.psum(returned.astype(jnp.bfloat16), 'section')]
    all_to_all x1 -> x0, blocking collectives: 32 us -> none  [per_device(): lax.all_to_all(partial_out.astype(jnp.bfloat16), 'dev', split_axis=0, con...]
    all_to_all x0 -> x1, waiting for transfers between devices: none -> 28.2 us  [per_device(): lax.all_to_all(partial_out.astype(jnp.bfloat16), 'dev', split_axis=0, con...]
    ppermute x0 -> x6, starting transfers between devices: none -> 9.13 us  [section_sum(): lax.ppermute(partial, 'section', [(i, (i + step) % sections) for i in ran...]
    gather x2 -> x0, local copies, waits for them, and re-layouts: 6.85 us -> none  [combine_rows(): routed = jnp.take(flat_out, target.reshape(-1), axis=0)]
    ppermute x0 -> x6, waiting for transfers between devices: none -> 6.56 us  [section_sum(): lax.ppermute(partial, 'section', [(i, (i + step) % sections) for i in ran...]
    all_to_all x0 -> x1, starting transfers between devices: none -> 4.68 us  [per_device(): lax.all_to_all(partial_out.astype(jnp.bfloat16), 'dev', split_axis=0, con...]
  transfers between devices with their start and end apart: 2 -> 7, of which waited for: 2 -> 3; matrix products, arithmetic and copies ran while one was open for 1% -> 4% of each run, Pallas kernels for 0% -> 0%
where the time goes in v1:
time: 125 us
  blocking collectives  37.6 us (30%)
  waiting for transfers between devices  34.8 us (28%)
  matrix products  22.8 us (18%)
  starting transfers between devices  13.8 us (11%)
  other arithmetic  9.78 us (8%)
  local copies, waits for them, and re-layouts  5.6 us (4%)
    all_to_all x1, blocking collectives, per_device(): lax.all_to_all(packed, 'dev', split_axis=0, concat_axis=0, tiled=True)  37.6 us
    all_to_all x1, waiting for transfers between devices, per_device(): lax.all_to_all(partial_out.astype(jnp.bfloat16), 'dev', split_axis=0, con...  28.2 us
    ppermute x6, starting transfers between devices, section_sum(): lax.ppermute(partial, 'section', [(i, (i + step) % sections) for i in ran...  9.13 us
    ppermute x6, waiting for transfers between devices, section_sum(): lax.ppermute(partial, 'section', [(i, (i + step) % sections) for i in ran...  6.56 us
    dot_general x1, matrix products, attend(): jnp.einsum('rhl,rtl->rht', query_latent, latent_cache, preferred_element_...  5.89 us
    dot_general x1, matrix products, expert_part(): jnp.einsum('secx,egfx->secgf', slot_rows, w_gate_up, preferred_element_ty...  4.8 us
    all_to_all x1, starting transfers between devices, per_device(): lax.all_to_all(partial_out.astype(jnp.bfloat16), 'dev', split_axis=0, con...  4.68 us
    reduce_sum x2, other arithmetic, rms_norm(): mean_square = jnp.mean(values * values, axis=-1, keepdims=True)  2.59 us
  transfers between devices with their start and end apart: 7, of which 3 were waited for; matrix products, arithmetic and copies ran while one was open for 4% of the time, Pallas kernels for 0%

profile of v1, /device:TPU:1, one launch (start us, length us, event | category | flops | bytes accessed | tf_op | source)
XLA Modules:
  0.0 124.7 jit_solution(4193376015978397141)
XLA Ops:
  0.6 1.4 %fusion.22 = f32[32]{0:T(128)S(1)} fusion(bf16[32,2048]{1,0:T(8,128)(2,1)} %param.17), kind=kLoop, calls=%fused_computation.34 | loop fusion | flops 196576 | bytes 131200 | tf_op jit(solution)/shard_map/reduce_sum | solution.py:16
  2.0 2.2 %convolution_convert_fusion.4 = bf16[32,768]{1,0:T(8,128)(2,1)} fusion(bf16[2048,768]{1,0:T(8,128)(2,1)S(1)} %copy-done, bf16[32,2048]{1,0:T(8,128)(2,1)} %param.17, f32[2048]{0:T(1024)} %param.19, f32[32]{0:T(128)S(1)} %add_rsqrt_fusion.2), kind=kOutput, calls=%fused_computation.16 | convolution fusion | flops 100950016 | bytes 3334272 | tf_op jit(solution)/shard_map/dot_general | solution.py:156
  4.2 1.5 %reshape.149 = bf16[32,4,192]{2,1,0:T(4,128)(2,1)} reshape(bf16[32,768]{1,0:T(8,128)(2,1)} %convolution_convert_fusion.4) | data formatting | bytes 98304 | tf_op jit(solution)/shard_map/reshape | solution.py:157
  5.8 0.9 slice_convert_fusion
  7.1 1.0 subtract_convert_fusion.1
  8.5 1.5 %fusion.61 = f32[32,4,256]{2,1,0:T(4,128)S(1)} fusion(bf16[32,64,256]{2,1,0:T(8,128)(2,1)} %param.28, bf16[32,4,32]{2,1,0:T(4,128)(2,1)S(1)} %get-tuple-element.8, bf16[32,4,32]{2,1,0:T(4,128)(2,1)S(1)} %get-tuple-element.7), kind=kOutput, calls=%fused_computation.99 | convolution fusion | flops 4227072 | bytes 1196032 | tf_op jit(solution)/shard_map/rhp,rpt->rht/dot_general | solution.py:100
  11.3 5.9 %fusion.70 = (f32[32,4]{1,0:T(8,128)S(1)}, f32[32,4,256]{2,1,0:T(4,128)S(1)}) fusion(f32[32,4,256]{2,1,0:T(4,128)S(1)} %fusion.61, bf16[32,256,512]{2,1,0:T(8,128)(2,1)} %param.27, bf16[32,4,512]{2,0,1:T(8,128)(2,1)S(1)} %fusion.13, pred[32,256]{1,0:T(8,128)(4,1)S(1)} %iota_compare_fusion.1), kind=kOutput, calls=%fused_computation.104 | convolution fusion | flops 33685376 | bytes 8790528 | tf_op jit(solution)/shard_map/rhl,rtl->rht/dot_general | solution.py:97
  17.5 1.2 fusion.12
  19.7 3.6 %collective-permute-start = (bf16[32,2048]{1,0:T(8,128)(2,1)S(1)}, bf16[32,2048]{1,0:T(8,128)(2,1)S(1)}, u32[]{:S(2)}, u32[]{:S(2)}) collective-permute-start(bf16[32,2048]{1,0:T(8,128)(2,1)S(1)} %convolution_convert_fusion.2), channel_id=1, source_target_pairs={{0,64},{32,96},{64,0},{96,32},{1,65},{33,97},{65,1},{97,33},{2,66}... | collective-permute-start | bytes 393224 | tf_op jit(solution)/shard_map/ppermute | solution.py:74
  23.7 2.4 %collective-permute-start.2 = (bf16[32,2048]{1,0:T(8,128)(2,1)S(1)}, bf16[32,2048]{1,0:T(8,128)(2,1)}, u32[]{:S(2)}, u32[]{:S(2)}) collective-permute-start(bf16[32,2048]{1,0:T(8,128)(2,1)S(1)} %convolution_convert_fusion.2), channel_id=1, source_target_pairs={{0,96},{32,0},{64,32},{96,64},{1,97},{33,1},{65,33},{97,65},{2,98}... | collective-permute-start | bytes 393224 | tf_op jit(solution)/shard_map/ppermute | solution.py:74
  27.3 1.2 convert_reduce_fusion
  31.5 1.2 fusion.26
  32.8 1.5 %convolution_convert_fusion = bf16[512,2048]{1,0:T(8,128)(2,1)S(1)} fusion(bf16[32,512]{1,0:T(8,128)(2,1)S(1)} %fusion.31, bf16[32,2048]{1,0:T(8,128)(2,1)S(1)} %get-tuple-element.6, f32[2048]{0:T(1024)} %param.29, f32[32]{0:T(128)S(1)} %add_rsqrt_fusion), kind=kOutput, calls=%fused_computation.2 | convolution fusion | flops 68419584 | bytes 2269312 | tf_op jit(solution)/shard_map/dot_general | solution.py:57
  34.2 37.6 %all_to_all.10 = bf16[32,2,8,2048]{3,2,1,0:T(8,128)(2,1)S(1)} all-to-all(bf16[32,2,8,2048]{3,2,1,0:T(8,128)(2,1)S(1)} %bitcast.71), channel_id=1, replica_groups=mesh['section'=4,'dev'=32] {'dev'}, dimensions={0} | all-to-all | bytes 4194304 | tf_op jit(solution)/shard_map/all_to_all | solution.py:192
  71.8 4.8 %fusion.7 = f32[32,2,8,2,352]{4,2,3,0,1:T(8,128)S(1)} fusion(bf16[2,2,352,2048]{3,2,1,0:T(8,128)(2,1)} %param.32, bf16[32,2,8,2048]{3,2,1,0:T(8,128)(2,1)S(1)} %all_to_all.10), kind=kOutput, calls=%fused_computation.8 | convolution fusion | flops 1476395008 | bytes 9306112 | tf_op jit(solution)/shard_map/secx,egfx->secgf/dot_general | solution.py:64
  76.6 1.3 %fusion.3 = bf16[32,2,8,2048]{3,2,0,1:T(8,128)(2,1)S(1)} fusion(bf16[2,352,2048]{2,1,0:T(8,128)(2,1)S(1)} %copy-done.13, f32[32,2,8,2,352]{4,2,3,0,1:T(8,128)S(1)} %fusion.7), kind=kOutput, calls=%fused_computation.5 | convolution fusion | flops 740327424 | bytes 6422528 | tf_op jit(solution)/shard_map/secf,efx->secx/dot_general | solution.py:68
  77.9 1.4 %copy.67 = bf16[32,2,8,2048]{3,2,1,0:T(8,128)(2,1)} copy(bf16[32,2,8,2048]{3,2,0,1:T(8,128)(2,1)S(1)} %fusion.3) | data formatting | bytes 4194304 | tf_op jit(solution)/shard_map/convert_element_type | solution.py:195
  79.3 4.7 %all-to-all-start.1 = ((bf16[32,2,8,2048]{3,2,1,0:T(8,128)(2,1)}), bf16[32,2,8,2048]{3,2,1,0:T(8,128)(2,1)}, u32[]{:S(2)}, u32[]{:S(2)}) async-start(bf16[32,2,8,2048]{3,2,1,0:T(8,128)(2,1)} %copy.67), calls=%async_computation.1 | async-start | bytes 4194304 | tf_op jit(solution)/shard_map/all_to_all | solution.py:194
  84.2 28.2 %all-to-all-done.1 = bf16[32,2,8,2048]{3,2,1,0:T(8,128)(2,1)} async-done(((bf16[32,2,8,2048]{3,2,1,0:T(8,128)(2,1)}), bf16[32,2,8,2048]{3,2,1,0:T(8,128)(2,1)}, u32[]{:S(2)}, u32[]{:S(2)}) %all-to-all-start.1) | async-done | bytes 2097184 | tf_op jit(solution)/shard_map/all_to_all | solution.py:194
  112.4 2.1 %fusion.41 = f32[64,2048]{1,0:T(8,128)S(1)} fusion(bf16[512,2048]{1,0:T(8,128)(2,1)} %bitcast.18, bf16[32,512]{1,0:T(8,128)(2,1)S(1)} %get-tuple-element.12, bf16[32,512]{1,0:T(8,128)(2,1)S(1)} %get-tuple-element.11), kind=kOutput, calls=%fused_computation.57 | convolution fusion | flops 134348800 | bytes 2686976 | tf_op jit(solution)/shard_map/dot_general | solution.py:90
  114.6 1.4 %collective-permute-start.4 = (bf16[32,2048]{1,0:T(8,128)(2,1)S(1)}, bf16[32,2048]{1,0:T(8,128)(2,1)S(1)}, u32[]{:S(2)}, u32[]{:S(2)}) collective-permute-start(bf16[32,2048]{1,0:T(8,128)(2,1)S(1)} %fusion.30), channel_id=1, source_target_pairs={{0,32},{32,64},{64,96},{96,0},{1,33},{33,65},{65,97},{97,1},{2,34}... | collective-permute-start | bytes 393224 | tf_op jit(solution)/shard_map/ppermute | solution.py:74
  116.0 1.3 %collective-permute-start.5 = (bf16[32,2048]{1,0:T(8,128)(2,1)S(1)}, bf16[32,2048]{1,0:T(8,128)(2,1)S(1)}, u32[]{:S(2)}, u32[]{:S(2)}) collective-permute-start(bf16[32,2048]{1,0:T(8,128)(2,1)S(1)} %fusion.30), channel_id=1, source_target_pairs={{0,96},{32,0},{64,32},{96,64},{1,97},{33,1},{65,33},{97,65},{2,98}... | collective-permute-start | bytes 393224 | tf_op jit(solution)/shard_map/ppermute | solution.py:74
  117.3 3.0 %collective-permute-done.3 = bf16[32,2048]{1,0:T(8,128)(2,1)S(1)} collective-permute-done((bf16[32,2048]{1,0:T(8,128)(2,1)S(1)}, bf16[32,2048]{1,0:T(8,128)(2,1)S(1)}, u32[]{:S(2)}, u32[]{:S(2)}) %collective-permute-start.3) | collective-permute-done | bytes 131104 | tf_op jit(solution)/shard_map/ppermute | solution.py:74
  120.3 3.6 %collective-permute-done.4 = bf16[32,2048]{1,0:T(8,128)(2,1)S(1)} collective-permute-done((bf16[32,2048]{1,0:T(8,128)(2,1)S(1)}, bf16[32,2048]{1,0:T(8,128)(2,1)S(1)}, u32[]{:S(2)}, u32[]{:S(2)}) %collective-permute-start.4) | collective-permute-done | bytes 131104 | tf_op jit(solution)/shard_map/ppermute | solution.py:74
  (74 shorter events, 9.3 us)
Async XLA Ops:
  0.0 2.0 %copy-start = (bf16[2048,768]{1,0:T(8,128)(2,1)S(1)}, bf16[2048,768]{1,0:T(8,128)(2,1)}, u32[]{:S(2)}) copy-start(bf16[2048,768]{1,0:T(8,128)(2,1)} %param.20) | copy-start | bytes 9437188
  0.0 6.8 %copy-start.1 = (bf16[32,2048]{1,0:T(8,128)(2,1)S(1)}, bf16[32,2048]{1,0:T(8,128)(2,1)}, u32[]{:S(2)}) copy-start(bf16[32,2048]{1,0:T(8,128)(2,1)} %param.17) | copy-start | bytes 393220
  0.0 6.8 %copy-start.8 = (f32[2048]{0:T(1024)S(1)}, f32[2048]{0:T(1024)}, u32[]{:S(2)}) copy-start(f32[2048]{0:T(1024)} %param.19) | copy-start | bytes 24580
  0.0 6.7 %copy-start.12 = (s32[32]{0:T(128)S(1)}, s32[32]{0:T(128)}, u32[]{:S(2)}) copy-start(s32[32]{0:T(128)} %param.18) | copy-start | bytes 388
  0.0 6.8 %copy-start.6 = (bf16[64,2048]{1,0:T(8,128)(2,1)S(1)}, bf16[64,2048]{1,0:T(8,128)(2,1)}, u32[]{:S(2)}) copy-start(bf16[64,2048]{1,0:T(8,128)(2,1)} %param.23) | copy-start | bytes 786436
  5.8 4.3 %copy-start.2 = (bf16[2048,512]{1,0:T(8,128)(2,1)S(1)}, bf16[2048,512]{1,0:T(8,128)(2,1)}, u32[]{:S(2)}) copy-start(bf16[2048,512]{1,0:T(8,128)(2,1)} %param.21) | copy-start | bytes 6291460
  5.8 5.2 %copy-start.11 = (f32[512]{0:T(512)S(1)}, f32[512]{0:T(512)}, u32[]{:S(2)}) copy-start(f32[512]{0:T(512)} %param.22) | copy-start | bytes 6148
  6.7 4.0 %copy-start.4 = (bf16[4,512,128]{2,1,0:T(8,128)(2,1)S(1)}, bf16[4,512,128]{2,1,0:T(8,128)(2,1)}, u32[]{:S(2)}) copy-start(bf16[4,512,128]{2,1,0:T(8,128)(2,1)} %param.24) | copy-start | bytes 1572868
  6.7 4.0 %slice-start.2 = ((bf16[32,4,192]{2,1,0:T(4,128)(2,1)}), bf16[32,4,128]{2,1,0:T(4,128)(2,1)S(1)}, s32[]{:S(2)}) async-start(bf16[32,4,192]{2,1,0:T(4,128)(2,1)} %reshape.149), calls=%async_computation.4 | async-start | bytes 65536 | tf_op jit(solution)/shard_map/slice | solution.py:162
  6.8 10.6 %slice-start = ((s8[8388608]{0:T(1024)(128)(4,1)}), s8[4194304]{0:T(1024)(128)(4,1)S(1)}, s32[]{:S(2)}) async-start(s8[8388608]{0:T(1024)(128)(4,1)} %bitcast.69), calls=%async_computation.2 | async-start | bytes 8388608
  11.3 6.2 %slice-start.1 = ((s8[8388608]{0:T(1024)(128)(4,1)}), s8[4194304]{0:T(1024)(128)(4,1)S(1)}, s32[]{:S(2)}) async-start(s8[8388608]{0:T(1024)(128)(4,1)} %bitcast.69), calls=%async_computation.3 | async-start | bytes 8388608
  17.5 1.3 %copy-start.5 = (bf16[4,512,128]{2,1,0:T(8,128)(2,1)S(1)}, bf16[4,512,128]{2,1,0:T(8,128)(2,1)}, u32[]{:S(2)}) copy-start(bf16[4,512,128]{2,1,0:T(8,128)(2,1)} %param.25) | copy-start | bytes 1572868
  17.5 1.8 %copy-start.3 = (bf16[512,2048]{1,0:T(8,128)(2,1)S(1)}, bf16[512,2048]{1,0:T(8,128)(2,1)}, u32[]{:S(2)}) copy-start(bf16[512,2048]{1,0:T(8,128)(2,1)} %param.26) | copy-start | bytes 6291460
  18.8 8.4 %copy-start.9 = (s32[32,6]{0,1:T(8,128)S(1)}, s32[32,6]{0,1:T(8,128)}, u32[]{:S(2)}) copy-start(s32[32,6]{0,1:T(8,128)} %param.30) | copy-start | bytes 2308
  19.7 11.1 %collective-permute-start = (bf16[32,2048]{1,0:T(8,128)(2,1)S(1)}, bf16[32,2048]{1,0:T(8,128)(2,1)S(1)}, u32[]{:S(2)}, u32[]{:S(2)}) collective-permute-start(bf16[32,2048]{1,0:T(8,128)(2,1)S(1)} %convolution_convert_fusion.2), channel_id=1, source_target_pairs={{0,64},{32,96},{64,0},{96,32},{1,65},{33,97},{65,1},{97,33},{2,66}... | collective-permute-start | bytes 393224 | tf_op jit(solution)/shard_map/ppermute | solution.py:74
  23.3 7.5 %collective-permute-start.1 = (bf16[32,2048]{1,0:T(8,128)(2,1)S(1)}, bf16[32,2048]{1,0:T(8,128)(2,1)}, u32[]{:S(2)}, u32[]{:S(2)}) collective-permute-start(bf16[32,2048]{1,0:T(8,128)(2,1)S(1)} %convolution_convert_fusion.2), channel_id=1, source_target_pairs={{0,32},{32,64},{64,96},{96,0},{1,33},{33,65},{65,97},{97,1},{2,34}... | collective-permute-start | bytes 393224 | tf_op jit(solution)/shard_map/ppermute | solution.py:74
  23.7 7.9 %collective-permute-start.2 = (bf16[32,2048]{1,0:T(8,128)(2,1)S(1)}, bf16[32,2048]{1,0:T(8,128)(2,1)}, u32[]{:S(2)}, u32[]{:S(2)}) collective-permute-start(bf16[32,2048]{1,0:T(8,128)(2,1)S(1)} %convolution_convert_fusion.2), channel_id=1, source_target_pairs={{0,96},{32,0},{64,32},{96,64},{1,97},{33,1},{65,33},{97,65},{2,98}... | collective-permute-start | bytes 393224 | tf_op jit(solution)/shard_map/ppermute | solution.py:74
  30.9 0.7 copy-start.7
  71.8 4.8 %copy-start.13 = (bf16[2,352,2048]{2,1,0:T(8,128)(2,1)S(1)}, bf16[2,352,2048]{2,1,0:T(8,128)(2,1)}, u32[]{:S(2)}) copy-start(bf16[2,352,2048]{2,1,0:T(8,128)(2,1)} %param.33) | copy-start | bytes 8650756
  79.3 4.7 %copy-start.10 = (f32[32,6]{0,1:T(8,128)S(1)}, f32[32,6]{0,1:T(8,128)}, u32[]{:S(2)}) copy-start(f32[32,6]{0,1:T(8,128)} %param.31) | copy-start | bytes 2308
  79.3 33.1 %all-to-all-start.1 = ((bf16[32,2,8,2048]{3,2,1,0:T(8,128)(2,1)}), bf16[32,2,8,2048]{3,2,1,0:T(8,128)(2,1)}, u32[]{:S(2)}, u32[]{:S(2)}) async-start(bf16[32,2,8,2048]{3,2,1,0:T(8,128)(2,1)} %copy.67), calls=%async_computation.1 | async-start | bytes 4194304 | tf_op jit(solution)/shard_map/all_to_all | solution.py:194
  114.5 5.8 %collective-permute-start.3 = (bf16[32,2048]{1,0:T(8,128)(2,1)S(1)}, bf16[32,2048]{1,0:T(8,128)(2,1)S(1)}, u32[]{:S(2)}, u32[]{:S(2)}) collective-permute-start(bf16[32,2048]{1,0:T(8,128)(2,1)S(1)} %fusion.30), channel_id=1, source_target_pairs={{0,64},{32,96},{64,0},{96,32},{1,65},{33,97},{65,1},{97,33},{2,66}... | collective-permute-start | bytes 393224 | tf_op jit(solution)/shard_map/ppermute | solution.py:74
  114.6 9.3 %collective-permute-start.4 = (bf16[32,2048]{1,0:T(8,128)(2,1)S(1)}, bf16[32,2048]{1,0:T(8,128)(2,1)S(1)}, u32[]{:S(2)}, u32[]{:S(2)}) collective-permute-start(bf16[32,2048]{1,0:T(8,128)(2,1)S(1)} %fusion.30), channel_id=1, source_target_pairs={{0,32},{32,64},{64,96},{96,0},{1,33},{33,65},{65,97},{97,1},{2,34}... | collective-permute-start | bytes 393224 | tf_op jit(solution)/shard_map/ppermute | solution.py:74
  116.0 7.9 %collective-permute-start.5 = (bf16[32,2048]{1,0:T(8,128)(2,1)S(1)}, bf16[32,2048]{1,0:T(8,128)(2,1)S(1)}, u32[]{:S(2)}, u32[]{:S(2)}) collective-permute-start(bf16[32,2048]{1,0:T(8,128)(2,1)S(1)} %fusion.30), channel_id=1, source_target_pairs={{0,96},{32,0},{64,32},{96,64},{1,97},{33,1},{65,33},{97,65},{2,98}... | collective-permute-start | bytes 393224 | tf_op jit(solution)/shard_map/ppermute | solution.py:74

commit v2 on v1

v2 whole, which is shorter than its diff:
```python
import jax
import jax.numpy as jnp
from jax import lax
from jax.experimental import pallas as pl
from jax.experimental.pallas import tpu as pltpu
from jax.sharding import PartitionSpec as P

EXPERTS = 64
MOST = 2
ROW_Q = 8
GROUP = 4


epsilon = 1e-06
far_below = -1e30


def rms_norm(values, norm_gain):
    mean_square = jnp.mean(values * values, axis=-1, keepdims=True)
    return values * lax.rsqrt(mean_square + epsilon) * norm_gain


def pack_rows(source, table):
    packed = lax.dot_general(
        table, source, (((0,), (0,)), ((), ())), preferred_element_type=jnp.float32
    )
    return packed.astype(jnp.bfloat16)


def expert_part(slot_rows, w_gate_up, w_down):
    gate_up = jnp.einsum(
        "secx,egfx->secgf", slot_rows, w_gate_up, preferred_element_type=jnp.float32
    )
    activated = (jax.nn.silu(gate_up[:, :, :, 0, :]) * gate_up[:, :, :, 1, :]).astype(jnp.bfloat16)
    return jnp.einsum("secf,efx->secx", activated, w_down, preferred_element_type=jnp.float32)


def section_sum(partial):
    sections = lax.axis_size("section")
    shifted = [
        lax.ppermute(partial, "section", [(i, (i + step) % sections) for i in range(sections)])
        for step in range(1, sections)
    ]
    held = [value.astype(jnp.float32) for value in [partial] + shifted]
    half = sections // 2
    pairs = [held[i] + held[i + half] for i in range(half)]
    return sum(pairs[1:], pairs[0])


def combine_rows(returned, mix):
    flat_out = returned.reshape(-1, returned.shape[-1])
    sums = jnp.dot(mix, flat_out, preferred_element_type=jnp.float32)
    half = mix.shape[0] // 2
    return sums[:half] + sums[half:]


def attend_kernel(
    hidden_ref, lengths_ref, attn_gain_ref, latent_gain_ref, ids_ref, weights_ref,
    w_query_hbm, w_latent_hbm, w_rope_hbm, w_key_up_hbm, latent_hbm, rope_hbm, w_value_up_hbm, w_out_hbm,
    partial_ref, table_ref, mix_ref,
    w_query, w_latent, w_rope, w_key_up, latent, rope, w_value_up, w_out,
    query_rows, turned_rows, mixed_rows, weight_sems, cache_sems,
):
    rows = hidden_ref.shape[0]
    heads, latent_width, nope_width = w_key_up.shape
    rope_width = w_rope.shape[0]
    slots = latent.shape[1]
    half = rope_width // 2
    head_width = nope_width + rope_width
    flat = rows * heads
    score_scale = head_width ** (-0.5)
    step_rows = GROUP
    steps = rows // step_rows
    tile = step_rows * heads

    early = [
        pltpu.make_async_copy(source, target, weight_sems.at[i])
        for i, (source, target) in enumerate(
            [
                (w_query_hbm, w_query),
                (w_key_up_hbm, w_key_up),
                (w_latent_hbm, w_latent),
                (w_rope_hbm, w_rope),
            ]
        )
    ]
    late = [
        pltpu.make_async_copy(source, target, weight_sems.at[len(early) + i])
        for i, (source, target) in enumerate([(w_value_up_hbm, w_value_up), (w_out_hbm, w_out)])
    ]
    cache = []
    for i in range(steps):
        span = pl.ds(i * step_rows, step_rows)
        cache.append(
            (
                pltpu.make_async_copy(latent_hbm.at[span], latent.at[span], cache_sems.at[i, 0]),
                pltpu.make_async_copy(rope_hbm.at[span], rope.at[span], cache_sems.at[i, 1]),
            )
        )
    for copy in early:
        copy.start()
    for pair in cache:
        for copy in pair:
            copy.start()
    for copy in late:
        copy.start()

    def count(shape, axis):
        return lax.broadcasted_iota(jnp.int32, shape, axis)

    slot_count = table_ref.shape[1]
    capacity = slot_count // EXPERTS
    slot_index = count((rows, slot_count), 1)
    slot_expert = slot_index // capacity
    slot_place = slot_index % capacity
    named = jnp.zeros((rows, slot_count), jnp.float32)
    weight = jnp.zeros((rows, slot_count), jnp.float32)
    for k in range(ids_ref.shape[1]):
        hit = ids_ref[:, k : k + 1] == slot_expert
        named = jnp.where(hit, 1.0, named)
        weight = jnp.where(hit, weights_ref[:, k : k + 1], weight)
    one, two = count((rows, rows), 0), count((rows, rows), 1)
    before = jnp.where((two < one) & (two // ROW_Q == one // ROW_Q), 1.0, 0.0)
    rank_in = jnp.dot(
        before.astype(jnp.bfloat16), named.astype(jnp.bfloat16), preferred_element_type=jnp.float32
    )
    wanted = (count((rows, slot_count), 0) // ROW_Q) * MOST + rank_in.astype(jnp.int32)
    taken = (slot_place == wanted) & (named > 0.0)
    table_ref[...] = jnp.where(taken, 1.0, 0.0).astype(jnp.bfloat16)
    weight = jnp.where(taken, weight, 0.0)
    upper = weight.astype(jnp.bfloat16)
    mix_ref[0:rows, :] = upper
    mix_ref[rows : 2 * rows, :] = (weight - upper.astype(jnp.float32)).astype(jnp.bfloat16)

    lengths = lengths_ref[...].astype(jnp.float32)
    repeat = jnp.where(count((flat, rows), 0) // heads == count((flat, rows), 1), 1.0, 0.0)
    flat_length = jnp.sum(repeat * lengths, axis=1, keepdims=True)
    same = jnp.where(one == two, 1.0, 0.0)
    row_length = jnp.sum(same * lengths, axis=1, keepdims=True)
    repeat = repeat.astype(jnp.bfloat16)
    place, other = count((flat, flat), 0), count((flat, flat), 1)
    order = jnp.where(place == (other % rows) * heads + other // rows, 1.0, 0.0).astype(jnp.bfloat16)
    back = jnp.where(other == (place % rows) * heads + place // rows, 1.0, 0.0).astype(jnp.bfloat16)
    frequency = jnp.exp(
        -jnp.log(10000.0) * count((1, half), 1).astype(jnp.float32) / half
    )
    angles = row_length * frequency
    cosine, sine_part = jnp.cos(angles), jnp.sin(angles)

    def turned(first_half, second):
        return jnp.concatenate(
            [first_half * cosine - second * sine_part, second * cosine + first_half * sine_part],
            axis=1,
        ).astype(jnp.bfloat16)

    values = hidden_ref[...].astype(jnp.float32)
    mean_square = jnp.mean(values * values, axis=1, keepdims=True)
    normed = (values * lax.rsqrt(mean_square + epsilon) * attn_gain_ref[...]).astype(jnp.bfloat16)

    early[0].wait()
    queries = jnp.dot(normed, w_query[...], preferred_element_type=jnp.float32).astype(jnp.bfloat16)
    early[1].wait()
    by_head, turned_by_head = [], []
    for h in range(heads):
        start = h * head_width
        nope = queries[:, start : start + nope_width]
        by_head.append(
            lax.dot_general(
                nope, w_key_up[h], (((1,), (1,)), ((), ())), preferred_element_type=jnp.float32
            ).astype(jnp.bfloat16)
        )
        middle = start + nope_width
        turned_by_head.append(
            turned(
                queries[:, middle : middle + half].astype(jnp.float32),
                queries[:, middle + half : middle + rope_width].astype(jnp.float32),
            )
        )
    query_rows[...] = jnp.dot(
        order, jnp.concatenate(by_head, axis=0), preferred_element_type=jnp.float32
    ).astype(jnp.bfloat16)
    turned_rows[...] = jnp.dot(
        order, jnp.concatenate(turned_by_head, axis=0), preferred_element_type=jnp.float32
    ).astype(jnp.bfloat16)

    early[2].wait()
    latent_raw = jnp.dot(normed, w_latent[...], preferred_element_type=jnp.float32)
    mean_square = jnp.mean(latent_raw * latent_raw, axis=1, keepdims=True)
    latent_new = (latent_raw * lax.rsqrt(mean_square + epsilon) * latent_gain_ref[...]).astype(
        jnp.bfloat16
    )
    early[3].wait()
    key_raw = lax.dot_general(
        normed, w_rope[...], (((1,), (1,)), ((), ())), preferred_element_type=jnp.float32
    )
    key_new = turned(key_raw[:, :half], key_raw[:, half:])
    latent_flat = jnp.dot(repeat, latent_new, preferred_element_type=jnp.float32)
    key_flat = jnp.dot(repeat, key_new, preferred_element_type=jnp.float32)
    self_score = (
        jnp.sum(query_rows[...].astype(jnp.float32) * latent_flat, axis=1, keepdims=True)
        + jnp.sum(turned_rows[...].astype(jnp.float32) * key_flat, axis=1, keepdims=True)
    ) * score_scale

    owner = count((tile, 1), 0) // heads
    places = count((tile, slots), 1).astype(jnp.float32)

    def scores_of(i):
        span = slice(i * tile, (i + 1) * tile)
        query, query_turned = query_rows[span, :], turned_rows[span, :]
        total = jnp.zeros((tile, slots), jnp.float32)
        for j in range(step_rows):
            row = i * step_rows + j
            part = lax.dot_general(
                query, latent[row], (((1,), (1,)), ((), ())), preferred_element_type=jnp.float32
            ) + jnp.dot(query_turned, rope[row], preferred_element_type=jnp.float32)
            total = jnp.where(owner == j, part, total)
        return total * score_scale

    def mix(i, scores):
        span = slice(i * tile, (i + 1) * tile)
        valid = places < flat_length[span]
        own = self_score[span]
        masked = jnp.where(valid, scores, far_below)
        peak = jnp.maximum(jnp.max(masked, axis=1, keepdims=True), own)
        weights = jnp.where(valid, jnp.exp(masked - peak), 0.0)
        self_weight = jnp.exp(own - peak)
        total = jnp.sum(weights, axis=1, keepdims=True) + self_weight
        probs = (weights / total).astype(jnp.bfloat16)
        prob_self = (self_weight / total).astype(jnp.bfloat16).astype(jnp.float32)
        mixed = jnp.zeros((tile, latent_width), jnp.float32)
        for j in range(step_rows):
            part = jnp.dot(probs, latent[i * step_rows + j], preferred_element_type=jnp.float32)
            mixed = jnp.where(owner == j, part, mixed)
        mixed_rows[span, :] = (mixed + prob_self * latent_flat[span]).astype(jnp.bfloat16)

    held = None
    for i in range(steps):
        for copy in cache[i]:
            copy.wait()
        scores = scores_of(i)
        if held is not None:
            mix(i - 1, held)
        held = scores
    mix(steps - 1, held)

    for copy in late:
        copy.wait()
    by_row = jnp.dot(back, mixed_rows[...], preferred_element_type=jnp.float32).astype(jnp.bfloat16)
    outs = [
        jnp.dot(
            by_row[h * rows : (h + 1) * rows], w_value_up[h], preferred_element_type=jnp.float32
        ).astype(jnp.bfloat16)
        for h in range(heads)
    ]
    partial_ref[...] = jnp.dot(
        jnp.concatenate(outs, axis=1), w_out[...], preferred_element_type=jnp.float32
    ).astype(jnp.bfloat16)


def attend_rows(
    hidden, lengths, attn_gain, latent_gain, expert_ids, route_weights,
    w_query, w_latent, w_rope_key, w_key_up, latent_cache, rope_cache, w_value_up, w_out,
):
    rows, model_width = hidden.shape
    heads, latent_width = w_key_up.shape[:2]
    capacity = rows // ROW_Q * MOST
    slot_count = EXPERTS * capacity
    big = (w_query, w_latent, w_rope_key, w_key_up, latent_cache, rope_cache, w_value_up, w_out)
    steps = rows // GROUP
    return pl.pallas_call(
        attend_kernel,
        out_shape=(
            jax.ShapeDtypeStruct((rows, model_width), jnp.bfloat16),
            jax.ShapeDtypeStruct((rows, slot_count), jnp.bfloat16),
            jax.ShapeDtypeStruct((2 * rows, slot_count), jnp.bfloat16),
        ),
        in_specs=[pl.BlockSpec(memory_space=pltpu.VMEM)] * 6
        + [pl.BlockSpec(memory_space=pl.ANY)] * len(big),
        out_specs=(pl.BlockSpec(memory_space=pltpu.VMEM),) * 3,
        scratch_shapes=[pltpu.VMEM(array.shape, array.dtype) for array in big]
        + [
            pltpu.VMEM((rows * heads, latent_width), jnp.bfloat16),
            pltpu.VMEM((rows * heads, w_rope_key.shape[0]), jnp.bfloat16),
            pltpu.VMEM((rows * heads, latent_width), jnp.bfloat16),
            pltpu.SemaphoreType.DMA((6,)),
            pltpu.SemaphoreType.DMA((steps, 2)),
        ],
        compiler_params=pltpu.CompilerParams(vmem_limit_bytes=40 << 20),
        name="attend_rows",
    )(
        hidden, lengths.reshape(1, rows), attn_gain.reshape(1, -1), latent_gain.reshape(1, -1),
        expert_ids, route_weights, *big,
    )


def per_device(
    hidden,
    lengths,
    attn_gain,
    w_query,
    w_latent,
    latent_gain,
    w_rope_key,
    w_key_up,
    w_value_up,
    w_out,
    latent_cache,
    rope_cache,
    ffn_gain,
    expert_ids,
    route_weights,
    w_gate_up,
    w_down,
):
    devices = lax.axis_size("dev")
    model_width = hidden.shape[1]
    partial_value, table, mix = attend_rows(
        hidden, lengths, attn_gain, latent_gain, expert_ids, route_weights,
        w_query, w_latent, w_rope_key, w_key_up, latent_cache, rope_cache, w_value_up, w_out,
    )
    middle = (hidden.astype(jnp.float32) + section_sum(partial_value)).astype(jnp.bfloat16)
    expert_in = rms_norm(middle.astype(jnp.float32), ffn_gain).astype(jnp.bfloat16)
    capacity = table.shape[1] // EXPERTS
    packed = pack_rows(expert_in, table).reshape(devices, -1, capacity, model_width)
    partial_out = expert_part(
        lax.all_to_all(packed, "dev", split_axis=0, concat_axis=0, tiled=True), w_gate_up, w_down
    )
    returned = lax.all_to_all(
        partial_out.astype(jnp.bfloat16), "dev", split_axis=0, concat_axis=0, tiled=True
    )
    routed = section_sum(combine_rows(returned, mix).astype(jnp.bfloat16))
    return (middle.astype(jnp.float32) + routed).astype(jnp.bfloat16)


def solution(mesh):
    in_specs = (
        P("dev", None),
        P("dev"),
        P(),
        P(None, "section"),
        P(),
        P(),
        P(),
        P("section", None, None),
        P("section", None, None),
        P("section", None),
        P("dev", None, None),
        P("dev", None, None),
        P(),
        P("dev", None),
        P("dev", None),
        P("dev", None, "section", None),
        P("dev", "section", None),
    )
    out_specs = P("dev", None)
    return jax.shard_map(
        per_device, mesh=mesh, in_specs=in_specs, out_specs=out_specs, check_vma=False
    )
```

time: 125 us -> 121 us (0.968)
  blocking collectives: 37.6 us -> 71 us
  waiting for transfers between devices: 34.8 us -> 12 us
  matrix products: 22.8 us -> 4.52 us
  Pallas kernels: 0 us -> 10.1 us
  other arithmetic: 9.78 us -> 1 us
  local copies, waits for them, and re-layouts: 5.6 us -> 14.2 us
  starting transfers between devices: 13.8 us -> 7.85 us
    all_to_all x0 -> x1, blocking collectives: none -> 31.9 us  [per_device(): lax.all_to_all(partial_out.astype(jnp.bfloat16), 'dev', split_axis=0, con...]
    all_to_all x1 -> x0, waiting for transfers between devices: 28.2 us -> none  [per_device(): lax.all_to_all(partial_out.astype(jnp.bfloat16), 'dev', split_axis=0, con...]
    dot_general x13 -> x2, matrix products: 16.7 us -> 1.24 us  [the longest x1 0.76 us: pack_rows(): lax.dot_general(table, source, (((0,), (0,)), ((), ())), preferred_elemen...]
    unnamed x32 -> x30, local copies, waits for them, and re-layouts: 1.01 us -> 14 us
    pallas_call x0 -> x1, Pallas kernels: none -> 10.1 us  [attend_rows(): pl.pallas_call(attend_kernel, out_shape=(jax.ShapeDtypeStruct((rows, mode...]
    ppermute x6, waiting for transfers between devices: 6.56 us -> 12 us  [section_sum(): lax.ppermute(partial, 'section', [(i, (i + step) % sections) for i in ran...]
    all_to_all x1 -> x0, starting transfers between devices: 4.68 us -> none  [per_device(): lax.all_to_all(partial_out.astype(jnp.bfloat16), 'dev', split_axis=0, con...]
    dot_general x1, matrix products: 4.8 us -> 2.02 us  [expert_part(): jnp.einsum('secx,egfx->secgf', slot_rows, w_gate_up, preferred_element_ty...]
  transfers between devices with their start and end apart: 7 -> 6, of which waited for: 3 -> 4; matrix products, arithmetic and copies ran while one was open for 4% -> 0% of each run, Pallas kernels for 0% -> 0%
where the time goes in v2:
time: 121 us
  blocking collectives  71 us (59%)
  local copies, waits for them, and re-layouts  14.2 us (12%)
  waiting for transfers between devices  12 us (10%)
  Pallas kernels  10.1 us (8%)
  starting transfers between devices  7.85 us (6%)
  matrix products  4.52 us (4%)
    all_to_all x1, blocking collectives, per_device(): lax.all_to_all(packed, 'dev', split_axis=0, concat_axis=0, tiled=True)  39.1 us
    all_to_all x1, blocking collectives, per_device(): lax.all_to_all(partial_out.astype(jnp.bfloat16), 'dev', split_axis=0, con...  31.9 us
    unnamed x30, local copies, waits for them, and re-layouts  14 us
    ppermute x6, waiting for transfers between devices, section_sum(): lax.ppermute(partial, 'section', [(i, (i + step) % sections) for i in ran...  12 us
    pallas_call x1, Pallas kernels, attend_rows(): pl.pallas_call(attend_kernel, out_shape=(jax.ShapeDtypeStruct((rows, mode...  10.1 us
    ppermute x6, starting transfers between devices, section_sum(): lax.ppermute(partial, 'section', [(i, (i + step) % sections) for i in ran...  7.85 us
  transfers between devices with their start and end apart: 6, of which 4 were waited for; matrix products, arithmetic and copies ran while one was open for 0% of the time, Pallas kernels for 0%

profile of v2, /device:TPU:1, one launch (start us, length us, event | category | flops | bytes accessed | tf_op | source)
XLA Modules:
  0.0 120.8 jit_solution(17361619639467794691)
XLA Ops:
  0.0 0.9 copy.27.ids_ref
  0.9 0.8 copy.28.weights_ref
  1.7 1.9 %copy-done.1 = bf16[2048,768]{1,0:T(8,128)(2,1)S(1)} copy-done((bf16[2048,768]{1,0:T(8,128)(2,1)S(1)}, bf16[2048,768]{1,0:T(8,128)(2,1)}, u32[]{:S(2)}) %copy-start.1) | copy-done | bytes 3145752
  3.6 1.6 %copy-done.2 = bf16[2048,512]{1,0:T(8,128)(2,1)S(1)} copy-done((bf16[2048,512]{1,0:T(8,128)(2,1)S(1)}, bf16[2048,512]{1,0:T(8,128)(2,1)}, u32[]{:S(2)}) %copy-start.2) | copy-done | bytes 2097176
  5.2 1.6 %copy-done.3 = bf16[512,2048]{1,0:T(8,128)(2,1)S(1)} copy-done((bf16[512,2048]{1,0:T(8,128)(2,1)S(1)}, bf16[512,2048]{1,0:T(8,128)(2,1)}, u32[]{:S(2)}) %copy-start.3) | copy-done | bytes 2097176
  6.8 1.2 %copy-done.4 = bf16[32,64,256]{2,1,0:T(8,128)(2,1)S(1)} copy-done((bf16[32,64,256]{2,1,0:T(8,128)(2,1)S(1)}, bf16[32,64,256]{2,1,0:T(8,128)(2,1)}, u32[]{:S(2)}) %copy-start.4) | copy-done | bytes 1048600
  8.0 1.0 copy-done.5
  9.0 1.0 copy-done.6
  10.1 0.9 copy-done.7
  11.0 0.9 copy-done.8
  11.9 0.7 copy-done.9
  14.0 10.1 %attend_rows.1 = (bf16[32,2048]{1,0:T(8,128)(2,1)S(1)}, bf16[32,512]{1,0:T(8,128)(2,1)S(1)}, bf16[64,512]{1,0:T(8,128)(2,1)S(1)}) custom-call(bf16[32,2048]{1,0:T(8,128)(2,1)S(1)} %copy-done.7, s32[1,32]{1,0:T(1,128)S(1)} %bitcast.46, f32[1,2048]{1,0:T(1,128)S(1)} %bitcast.44, f32[1,512]{1,0:T(1,128)S(1)} %bitcast.45, s32[32,6]{1,0:T(8,128)S(1)} %copy.27.ids_ref, ...), custom_call_target="tpu_custom_call" | custom-call | tf_op jit(solution)/shard_map/attend_rows/pallas_call | solution.py:270
  24.1 3.4 %collective-permute-start.2 = (bf16[32,2048]{1,0:T(8,128)(2,1)S(1)}, bf16[32,2048]{1,0:T(8,128)(2,1)S(1)}, u32[]{:S(2)}, u32[]{:S(2)}) collective-permute-start(bf16[32,2048]{1,0:T(8,128)(2,1)S(1)} %get-tuple-element.8), channel_id=1, source_target_pairs={{0,96},{32,0},{64,32},{96,64},{1,97},{33,1},{65,33},{97,65},{2,98}... | collective-permute-start | bytes 393224 | tf_op jit(solution)/shard_map/ppermute | solution.py:41
  27.5 1.7 %collective-permute-start = (bf16[32,2048]{1,0:T(8,128)(2,1)S(1)}, bf16[32,2048]{1,0:T(8,128)(2,1)S(1)}, u32[]{:S(2)}, u32[]{:S(2)}) collective-permute-start(bf16[32,2048]{1,0:T(8,128)(2,1)S(1)} %get-tuple-element.8), channel_id=1, source_target_pairs={{0,64},{32,96},{64,0},{96,32},{1,65},{33,97},{65,1},{97,33},{2,66}... | collective-permute-start | bytes 393224 | tf_op jit(solution)/shard_map/ppermute | solution.py:41
  29.6 5.0 %collective-permute-done.1 = bf16[32,2048]{1,0:T(8,128)(2,1)S(1)} collective-permute-done((bf16[32,2048]{1,0:T(8,128)(2,1)S(1)}, bf16[32,2048]{1,0:T(8,128)(2,1)S(1)}, u32[]{:S(2)}, u32[]{:S(2)}) %collective-permute-start.1) | collective-permute-done | bytes 131104 | tf_op jit(solution)/shard_map/ppermute | solution.py:41
  34.9 0.8 convolution_convert_fusion
  35.6 39.1 %all_to_all.10 = bf16[32,2,8,2048]{3,2,1,0:T(8,128)(2,1)S(1)} all-to-all(bf16[32,2,8,2048]{3,2,1,0:T(8,128)(2,1)S(1)} %bitcast.48), channel_id=1, replica_groups=mesh['section'=4,'dev'=32] {'dev'}, dimensions={0} | all-to-all | bytes 4194304 | tf_op jit(solution)/shard_map/all_to_all | solution.py:326
  74.7 2.0 %fusion.7 = f32[32,2,8,2,352]{4,2,3,0,1:T(8,128)S(1)} fusion(bf16[2,2,352,2048]{3,2,1,0:T(8,128)(2,1)S(1)} %copy-done.13, bf16[32,2,8,2048]{3,2,1,0:T(8,128)(2,1)S(1)} %all_to_all.10), kind=kOutput, calls=%fused_computation.7 | convolution fusion | flops 1476395008 | bytes 9306112 | tf_op jit(solution)/shard_map/secx,egfx->secgf/dot_general | solution.py:31
  76.8 1.3 %fusion.3 = bf16[32,2,8,2048]{3,2,0,1:T(8,128)(2,1)S(1)} fusion(bf16[2,352,2048]{2,1,0:T(8,128)(2,1)S(1)} %copy-done, f32[32,2,8,2,352]{4,2,3,0,1:T(8,128)S(1)} %fusion.7), kind=kOutput, calls=%fused_computation.5 | convolution fusion | flops 740327424 | bytes 6422528 | tf_op jit(solution)/shard_map/secf,efx->secx/dot_general | solution.py:35
  78.3 31.9 %all_to_all.11 = bf16[32,2,8,2048]{3,2,1,0:T(8,128)(2,1)S(1)} all-to-all(bf16[32,2,8,2048]{3,2,1,0:T(8,128)(2,1)S(1)} %copy.31), channel_id=1, replica_groups=mesh['section'=4,'dev'=32] {'dev'}, dimensions={0} | all-to-all | bytes 4194304 | tf_op jit(solution)/shard_map/all_to_all | solution.py:328
  110.8 1.6 %collective-permute-start.3 = (bf16[32,2048]{1,0:T(8,128)(2,1)S(1)}, bf16[32,2048]{1,0:T(8,128)(2,1)S(1)}, u32[]{:S(2)}, u32[]{:S(2)}) collective-permute-start(bf16[32,2048]{1,0:T(8,128)(2,1)S(1)} %fusion.20), channel_id=1, source_target_pairs={{0,64},{32,96},{64,0},{96,32},{1,65},{33,97},{65,1},{97,33},{2,66}... | collective-permute-start | bytes 393224 | tf_op jit(solution)/shard_map/ppermute | solution.py:41
  112.4 1.0 collective-permute-start.5
  113.4 6.3 %collective-permute-done.4 = bf16[32,2048]{1,0:T(8,128)(2,1)S(1)} collective-permute-done((bf16[32,2048]{1,0:T(8,128)(2,1)S(1)}, bf16[32,2048]{1,0:T(8,128)(2,1)S(1)}, u32[]{:S(2)}, u32[]{:S(2)}) %collective-permute-start.4) | collective-permute-done | bytes 131104 | tf_op jit(solution)/shard_map/ppermute | solution.py:41
  120.0 0.7 fusion.19
  (30 shorter events, 3.1 us)
Async XLA Ops:
  0.0 76.8 %copy-start = (bf16[2,352,2048]{2,1,0:T(8,128)(2,1)S(1)}, bf16[2,352,2048]{2,1,0:T(8,128)(2,1)}, u32[]{:S(2)}) copy-start(bf16[2,352,2048]{2,1,0:T(8,128)(2,1)} %param.33) | copy-start | bytes 8650756
  1.7 1.9 %copy-start.1 = (bf16[2048,768]{1,0:T(8,128)(2,1)S(1)}, bf16[2048,768]{1,0:T(8,128)(2,1)}, u32[]{:S(2)}) copy-start(bf16[2048,768]{1,0:T(8,128)(2,1)} %w_query_hbm.1) | copy-start | bytes 9437188
  3.6 1.6 %copy-start.2 = (bf16[2048,512]{1,0:T(8,128)(2,1)S(1)}, bf16[2048,512]{1,0:T(8,128)(2,1)}, u32[]{:S(2)}) copy-start(bf16[2048,512]{1,0:T(8,128)(2,1)} %w_latent_hbm.1) | copy-start | bytes 6291460
  5.2 1.6 %copy-start.3 = (bf16[512,2048]{1,0:T(8,128)(2,1)S(1)}, bf16[512,2048]{1,0:T(8,128)(2,1)}, u32[]{:S(2)}) copy-start(bf16[512,2048]{1,0:T(8,128)(2,1)} %w_out_hbm.1) | copy-start | bytes 6291460
  6.8 1.2 %copy-start.4 = (bf16[32,64,256]{2,1,0:T(8,128)(2,1)S(1)}, bf16[32,64,256]{2,1,0:T(8,128)(2,1)}, u32[]{:S(2)}) copy-start(bf16[32,64,256]{2,1,0:T(8,128)(2,1)} %rope_hbm.1) | copy-start | bytes 3145732
  8.0 1.0 copy-start.5
  9.0 1.0 copy-start.6
  10.1 0.9 copy-start.7
  11.0 0.9 copy-start.8
  11.9 0.7 copy-start.9
  12.6 0.7 copy-start.10
  13.3 0.7 copy-start.11
  14.0 20.9 %copy-start.12 = (f32[2048]{0:T(1024)S(1)}, f32[2048]{0:T(1024)}, u32[]{:S(2)}) copy-start(f32[2048]{0:T(1024)} %param.29) | copy-start | bytes 24580
  24.1 5.5 %collective-permute-start.2 = (bf16[32,2048]{1,0:T(8,128)(2,1)S(1)}, bf16[32,2048]{1,0:T(8,128)(2,1)S(1)}, u32[]{:S(2)}, u32[]{:S(2)}) collective-permute-start(bf16[32,2048]{1,0:T(8,128)(2,1)S(1)} %get-tuple-element.8), channel_id=1, source_target_pairs={{0,96},{32,0},{64,32},{96,64},{1,97},{33,1},{65,33},{97,65},{2,98}... | collective-permute-start | bytes 393224 | tf_op jit(solution)/shard_map/ppermute | solution.py:41
  27.5 7.2 %collective-permute-start.1 = (bf16[32,2048]{1,0:T(8,128)(2,1)S(1)}, bf16[32,2048]{1,0:T(8,128)(2,1)S(1)}, u32[]{:S(2)}, u32[]{:S(2)}) collective-permute-start(bf16[32,2048]{1,0:T(8,128)(2,1)S(1)} %get-tuple-element.8), channel_id=1, source_target_pairs={{0,32},{32,64},{64,96},{96,0},{1,33},{33,65},{65,97},{97,1},{2,34}... | collective-permute-start | bytes 393224 | tf_op jit(solution)/shard_map/ppermute | solution.py:41
  27.5 7.2 %collective-permute-start = (bf16[32,2048]{1,0:T(8,128)(2,1)S(1)}, bf16[32,2048]{1,0:T(8,128)(2,1)S(1)}, u32[]{:S(2)}, u32[]{:S(2)}) collective-permute-start(bf16[32,2048]{1,0:T(8,128)(2,1)S(1)} %get-tuple-element.8), channel_id=1, source_target_pairs={{0,64},{32,96},{64,0},{96,32},{1,65},{33,97},{65,1},{97,33},{2,66}... | collective-permute-start | bytes 393224 | tf_op jit(solution)/shard_map/ppermute | solution.py:41
  34.9 39.9 %copy-start.13 = (bf16[2,2,352,2048]{3,2,1,0:T(8,128)(2,1)S(1)}, bf16[2,2,352,2048]{3,2,1,0:T(8,128)(2,1)}, u32[]{:S(2)}) copy-start(bf16[2,2,352,2048]{3,2,1,0:T(8,128)(2,1)} %param.32) | copy-start | bytes 17301508
  110.7 9.1 %collective-permute-start.4 = (bf16[32,2048]{1,0:T(8,128)(2,1)S(1)}, bf16[32,2048]{1,0:T(8,128)(2,1)S(1)}, u32[]{:S(2)}, u32[]{:S(2)}) collective-permute-start(bf16[32,2048]{1,0:T(8,128)(2,1)S(1)} %fusion.20), channel_id=1, source_target_pairs={{0,32},{32,64},{64,96},{96,0},{1,33},{33,65},{65,97},{97,1},{2,34}... | collective-permute-start | bytes 393224 | tf_op jit(solution)/shard_map/ppermute | solution.py:41
  110.8 9.0 %collective-permute-start.3 = (bf16[32,2048]{1,0:T(8,128)(2,1)S(1)}, bf16[32,2048]{1,0:T(8,128)(2,1)S(1)}, u32[]{:S(2)}, u32[]{:S(2)}) collective-permute-start(bf16[32,2048]{1,0:T(8,128)(2,1)S(1)} %fusion.20), channel_id=1, source_target_pairs={{0,64},{32,96},{64,0},{96,32},{1,65},{33,97},{65,1},{97,33},{2,66}... | collective-permute-start | bytes 393224 | tf_op jit(solution)/shard_map/ppermute | solution.py:41
  112.4 7.6 %collective-permute-start.5 = (bf16[32,2048]{1,0:T(8,128)(2,1)S(1)}, bf16[32,2048]{1,0:T(8,128)(2,1)S(1)}, u32[]{:S(2)}, u32[]{:S(2)}) collective-permute-start(bf16[32,2048]{1,0:T(8,128)(2,1)S(1)} %fusion.20), channel_id=1, source_target_pairs={{0,96},{32,0},{64,32},{96,64},{1,97},{33,1},{65,33},{97,65},{2,98}... | collective-permute-start | bytes 393224 | tf_op jit(solution)/shard_map/ppermute | solution.py:41

commit v3 on v2

--- a/solution.py
+++ b/solution.py
@@ -54,13 +54,16 @@
     return sums[:half] + sums[half:]
 
 
-def attend_kernel(
-    hidden_ref, lengths_ref, attn_gain_ref, latent_gain_ref, ids_ref, weights_ref,
-    w_query_hbm, w_latent_hbm, w_rope_hbm, w_key_up_hbm, latent_hbm, rope_hbm, w_value_up_hbm, w_out_hbm,
-    partial_ref, table_ref, mix_ref,
-    w_query, w_latent, w_rope, w_key_up, latent, rope, w_value_up, w_out,
-    query_rows, turned_rows, mixed_rows, weight_sems, cache_sems,
-):
+def attend_kernel(*refs):
+    sources, rest = refs[:14], refs[14:]
+    partial_ref, table_ref, mix_ref = rest[:3]
+    held_refs, rest = rest[3:17], rest[17:]
+    query_rows, turned_rows, mixed_rows, load_sems, cache_sems = rest
+    (
+        hidden_ref, lengths_ref, attn_gain_ref, latent_gain_ref, ids_ref, weights_ref,
+        w_query, w_key_up, w_latent, w_rope, w_value_up, w_out, latent, rope,
+    ) = held_refs
+    latent_hbm, rope_hbm = sources[12:]
     rows = hidden_ref.shape[0]
     heads, latent_width, nope_width = w_key_up.shape
     rope_width = w_rope.shape[0]
@@ -73,21 +76,11 @@
     steps = rows // step_rows
     tile = step_rows * heads
 
-    early = [
-        pltpu.make_async_copy(source, target, weight_sems.at[i])
-        for i, (source, target) in enumerate(
-            [
-                (w_query_hbm, w_query),
-                (w_key_up_hbm, w_key_up),
-                (w_latent_hbm, w_latent),
-                (w_rope_hbm, w_rope),
-            ]
-        )
+    loads = [
+        pltpu.make_async_copy(source, target, load_sems.at[i])
+        for i, (source, target) in enumerate(zip(sources[:12], held_refs[:12]))
     ]
-    late = [
-        pltpu.make_async_copy(source, target, weight_sems.at[len(early) + i])
-        for i, (source, target) in enumerate([(w_value_up_hbm, w_value_up), (w_out_hbm, w_out)])
-    ]
+    small, early, late = loads[:6], loads[6:10], loads[10:]
     cache = []
     for i in range(steps):
         span = pl.ds(i * step_rows, step_rows)
@@ -97,7 +90,7 @@
                 pltpu.make_async_copy(rope_hbm.at[span], rope.at[span], cache_sems.at[i, 1]),
             )
         )
-    for copy in early:
+    for copy in small + early:
         copy.start()
     for pair in cache:
         for copy in pair:
@@ -108,6 +101,14 @@
     def count(shape, axis):
         return lax.broadcasted_iota(jnp.int32, shape, axis)
 
+    one, two = count((rows, rows), 0), count((rows, rows), 1)
+    same = jnp.where(one == two, 1.0, 0.0)
+
+    def column(row):
+        return jnp.sum(same * row.astype(jnp.float32), axis=1, keepdims=True)
+
+    for copy in small:
+        copy.wait()
     slot_count = table_ref.shape[1]
     capacity = slot_count // EXPERTS
     slot_index = count((rows, slot_count), 1)
@@ -115,11 +116,10 @@
     slot_place = slot_index % capacity
     named = jnp.zeros((rows, slot_count), jnp.float32)
     weight = jnp.zeros((rows, slot_count), jnp.float32)
-    for k in range(ids_ref.shape[1]):
-        hit = ids_ref[:, k : k + 1] == slot_expert
+    for k in range(ids_ref.shape[0]):
+        hit = column(ids_ref[k : k + 1, :]).astype(jnp.int32) == slot_expert
         named = jnp.where(hit, 1.0, named)
-        weight = jnp.where(hit, weights_ref[:, k : k + 1], weight)
-    one, two = count((rows, rows), 0), count((rows, rows), 1)
+        weight = jnp.where(hit, column(weights_ref[k : k + 1, :]), weight)
     before = jnp.where((two < one) & (two // ROW_Q == one // ROW_Q), 1.0, 0.0)
     rank_in = jnp.dot(
         before.astype(jnp.bfloat16), named.astype(jnp.bfloat16), preferred_element_type=jnp.float32
@@ -135,8 +135,7 @@
     lengths = lengths_ref[...].astype(jnp.float32)
     repeat = jnp.where(count((flat, rows), 0) // heads == count((flat, rows), 1), 1.0, 0.0)
     flat_length = jnp.sum(repeat * lengths, axis=1, keepdims=True)
-    same = jnp.where(one == two, 1.0, 0.0)
-    row_length = jnp.sum(same * lengths, axis=1, keepdims=True)
+    row_length = column(lengths)
     repeat = repeat.astype(jnp.bfloat16)
     place, other = count((flat, flat), 0), count((flat, flat), 1)
     order = jnp.where(place == (other % rows) * heads + other // rows, 1.0, 0.0).astype(jnp.bfloat16)
@@ -265,7 +264,11 @@
     heads, latent_width = w_key_up.shape[:2]
     capacity = rows // ROW_Q * MOST
     slot_count = EXPERTS * capacity
-    big = (w_query, w_latent, w_rope_key, w_key_up, latent_cache, rope_cache, w_value_up, w_out)
+    sources = (
+        hidden, lengths.reshape(1, rows), attn_gain.reshape(1, -1), latent_gain.reshape(1, -1),
+        expert_ids.T, route_weights.T, w_query, w_key_up, w_latent, w_rope_key, w_value_up, w_out,
+        latent_cache, rope_cache,
+    )
     steps = rows // GROUP
     return pl.pallas_call(
         attend_kernel,
@@ -274,23 +277,19 @@
             jax.ShapeDtypeStruct((rows, slot_count), jnp.bfloat16),
             jax.ShapeDtypeStruct((2 * rows, slot_count), jnp.bfloat16),
         ),
-        in_specs=[pl.BlockSpec(memory_space=pltpu.VMEM)] * 6
-        + [pl.BlockSpec(memory_space=pl.ANY)] * len(big),
+        in_specs=[pl.BlockSpec(memory_space=pltpu.HBM)] * len(sources),
         out_specs=(pl.BlockSpec(memory_space=pltpu.VMEM),) * 3,
-        scratch_shapes=[pltpu.VMEM(array.shape, array.dtype) for array in big]
+        scratch_shapes=[pltpu.VMEM(array.shape, array.dtype) for array in sources]
         + [
             pltpu.VMEM((rows * heads, latent_width), jnp.bfloat16),
             pltpu.VMEM((rows * heads, w_rope_key.shape[0]), jnp.bfloat16),
             pltpu.VMEM((rows * heads, latent_width), jnp.bfloat16),
-            pltpu.SemaphoreType.DMA((6,)),
+            pltpu.SemaphoreType.DMA((12,)),
             pltpu.SemaphoreType.DMA((steps, 2)),
         ],
         compiler_params=pltpu.CompilerParams(vmem_limit_bytes=40 << 20),
         name="attend_rows",
-    )(
-        hidden, lengths.reshape(1, rows), attn_gain.reshape(1, -1), latent_gain.reshape(1, -1),
-        expert_ids, route_weights, *big,
-    )
+    )(*[pltpu.with_memory_space_constraint(array, pltpu.HBM) for array in sources])
 
 
 def per_device(

time: 121 us -> 109 us (0.901)
  local copies, waits for them, and re-layouts: 14.2 us -> 0.26 us
  Pallas kernels: 10.1 us -> 11.8 us
    unnamed x30 -> x8, local copies, waits for them, and re-layouts: 14 us -> 0.02 us
    pallas_call x1, Pallas kernels: 10.1 us -> 11.8 us  [attend_rows(): pl.pallas_call(attend_kernel, out_shape=(jax.ShapeDtypeStruct((rows, mode...]
where the time goes in v3:
time: 109 us; the launch traced here: 108 us
  blocking collectives  71 us (65%)
  waiting for transfers between devices  12 us (11%)
  Pallas kernels  11.8 us (11%)
  starting transfers between devices  7.85 us (7%)
  matrix products  4.44 us (4%)
    all_to_all x1, blocking collectives, per_device(): lax.all_to_all(packed, 'dev', split_axis=0, concat_axis=0, tiled=True)  39.1 us
    all_to_all x1, blocking collectives, per_device(): lax.all_to_all(partial_out.astype(jnp.bfloat16), 'dev', split_axis=0, con...  31.9 us
    ppermute x6, waiting for transfers between devices, section_sum(): lax.ppermute(partial, 'section', [(i, (i + step) % sections) for i in ran...  12 us
    pallas_call x1, Pallas kernels, attend_rows(): pl.pallas_call(attend_kernel, out_shape=(jax.ShapeDtypeStruct((rows, mode...  11.8 us
    ppermute x6, starting transfers between devices, section_sum(): lax.ppermute(partial, 'section', [(i, (i + step) % sections) for i in ran...  7.85 us
  transfers between devices with their start and end apart: 6, of which 4 were waited for; matrix products, arithmetic and copies ran while one was open for 0% of the time, Pallas kernels for 0%

profile of v3, /device:TPU:1, one launch (start us, length us, event | category | flops | bytes accessed | tf_op | source)
XLA Modules:
  0.0 108.5 jit_solution(4638369995656143707)
XLA Ops:
  0.0 11.8 %attend_rows.1 = (bf16[32,2048]{1,0:T(8,128)(2,1)S(1)}, bf16[32,512]{1,0:T(8,128)(2,1)S(1)}, bf16[64,512]{1,0:T(8,128)(2,1)S(1)}) custom-call(bf16[32,2048]{1,0:T(8,128)(2,1)} %refs_0_.1, s32[1,32]{1,0:T(1,128)} %bitcast.52, f32[1,2048]{1,0:T(1,128)} %bitcast.48, f32[1,512]{1,0:T(1,128)} %bitcast.51, s32[6,32]{1,0:T(8,128)} %bitcast.49, f32[6,32]{1,0:T(8,128)} %bitcast.50, ...), custom_call_target="tpu_custom_call" | custom-call | tf_op jit(solution)/shard_map/attend_rows/pallas_call | solution.py:273
  11.8 3.4 %collective-permute-start.2 = (bf16[32,2048]{1,0:T(8,128)(2,1)S(1)}, bf16[32,2048]{1,0:T(8,128)(2,1)S(1)}, u32[]{:S(2)}, u32[]{:S(2)}) collective-permute-start(bf16[32,2048]{1,0:T(8,128)(2,1)S(1)} %get-tuple-element.8), channel_id=1, source_target_pairs={{0,96},{32,0},{64,32},{96,64},{1,97},{33,1},{65,33},{97,65},{2,98}... | collective-permute-start | bytes 393224 | tf_op jit(solution)/shard_map/ppermute | solution.py:41
  15.2 0.0 collective-permute-start.1
  15.2 1.7 %collective-permute-start = (bf16[32,2048]{1,0:T(8,128)(2,1)S(1)}, bf16[32,2048]{1,0:T(8,128)(2,1)S(1)}, u32[]{:S(2)}, u32[]{:S(2)}) collective-permute-start(bf16[32,2048]{1,0:T(8,128)(2,1)S(1)} %get-tuple-element.8), channel_id=1, source_target_pairs={{0,64},{32,96},{64,0},{96,32},{1,65},{33,97},{65,1},{97,33},{2,66}... | collective-permute-start | bytes 393224 | tf_op jit(solution)/shard_map/ppermute | solution.py:41
  16.9 0.4 collective-permute-done.2
  17.4 5.0 %collective-permute-done.1 = bf16[32,2048]{1,0:T(8,128)(2,1)S(1)} collective-permute-done((bf16[32,2048]{1,0:T(8,128)(2,1)S(1)}, bf16[32,2048]{1,0:T(8,128)(2,1)S(1)}, u32[]{:S(2)}, u32[]{:S(2)}) %collective-permute-start.1) | collective-permute-done | bytes 131104 | tf_op jit(solution)/shard_map/ppermute | solution.py:41
  22.4 0.0 collective-permute-done
  22.4 0.0 copy-done.1
  22.4 0.2 fusion.16
  22.6 0.0 copy-start.3
  22.6 0.8 convolution_convert_fusion
  23.4 39.1 %all_to_all.10 = bf16[32,2,8,2048]{3,2,1,0:T(8,128)(2,1)S(1)} all-to-all(bf16[32,2,8,2048]{3,2,1,0:T(8,128)(2,1)S(1)} %bitcast.47), channel_id=1, replica_groups=mesh['section'=4,'dev'=32] {'dev'}, dimensions={0} | all-to-all | bytes 4194304 | tf_op jit(solution)/shard_map/all_to_all | solution.py:325
  62.5 1.9 %fusion.7 = f32[32,2,8,2,352]{4,2,3,0,1:T(8,128)S(1)} fusion(bf16[2,2,352,2048]{3,2,1,0:T(8,128)(2,1)S(1)} %copy-done.3, bf16[32,2,8,2048]{3,2,1,0:T(8,128)(2,1)S(1)} %all_to_all.10), kind=kOutput, calls=%fused_computation.7 | convolution fusion | flops 1476395008 | bytes 9306112 | tf_op jit(solution)/shard_map/secx,egfx->secgf/dot_general | solution.py:31
  64.4 1.3 %fusion.3 = bf16[32,2,8,2048]{3,2,0,1:T(8,128)(2,1)S(1)} fusion(bf16[2,352,2048]{2,1,0:T(8,128)(2,1)S(1)} %copy-done, f32[32,2,8,2,352]{4,2,3,0,1:T(8,128)S(1)} %fusion.7), kind=kOutput, calls=%fused_computation.5 | convolution fusion | flops 740327424 | bytes 6422528 | tf_op jit(solution)/shard_map/secf,efx->secx/dot_general | solution.py:35
  65.7 0.2 copy.25
  65.9 31.9 %all_to_all.11 = bf16[32,2,8,2048]{3,2,1,0:T(8,128)(2,1)S(1)} all-to-all(bf16[32,2,8,2048]{3,2,1,0:T(8,128)(2,1)S(1)} %copy.25), channel_id=1, replica_groups=mesh['section'=4,'dev'=32] {'dev'}, dimensions={0} | all-to-all | bytes 4194304 | tf_op jit(solution)/shard_map/all_to_all | solution.py:327
  97.8 0.5 fusion.25
  98.4 0.1 collective-permute-start.4
  98.4 1.6 %collective-permute-start.3 = (bf16[32,2048]{1,0:T(8,128)(2,1)S(1)}, bf16[32,2048]{1,0:T(8,128)(2,1)S(1)}, u32[]{:S(2)}, u32[]{:S(2)}) collective-permute-start(bf16[32,2048]{1,0:T(8,128)(2,1)S(1)} %fusion.20), channel_id=1, source_target_pairs={{0,64},{32,96},{64,0},{96,32},{1,65},{33,97},{65,1},{97,33},{2,66}... | collective-permute-start | bytes 393224 | tf_op jit(solution)/shard_map/ppermute | solution.py:41
  100.1 1.1 collective-permute-start.5
  101.1 6.3 %collective-permute-done.4 = bf16[32,2048]{1,0:T(8,128)(2,1)S(1)} collective-permute-done((bf16[32,2048]{1,0:T(8,128)(2,1)S(1)}, bf16[32,2048]{1,0:T(8,128)(2,1)S(1)}, u32[]{:S(2)}, u32[]{:S(2)}) %collective-permute-start.4) | collective-permute-done | bytes 131104 | tf_op jit(solution)/shard_map/ppermute | solution.py:41
  107.4 0.0 collective-permute-done.3
  107.4 0.3 collective-permute-done.5
  107.7 0.8 fusion.19
  (8 shorter events, 0.0 us)
Async XLA Ops:
  0.0 64.4 %copy-start = (bf16[2,352,2048]{2,1,0:T(8,128)(2,1)S(1)}, bf16[2,352,2048]{2,1,0:T(8,128)(2,1)}, u32[]{:S(2)}) copy-start(bf16[2,352,2048]{2,1,0:T(8,128)(2,1)} %param.33) | copy-start | bytes 8650756
  0.0 22.4 %copy-start.1 = (bf16[32,2048]{1,0:T(8,128)(2,1)S(1)}, bf16[32,2048]{1,0:T(8,128)(2,1)}, u32[]{:S(2)}) copy-start(bf16[32,2048]{1,0:T(8,128)(2,1)} %refs_0_.1) | copy-start | bytes 393220
  0.0 22.6 %copy-start.2 = (f32[2048]{0:T(1024)S(1)}, f32[2048]{0:T(1024)}, u32[]{:S(2)}) copy-start(f32[2048]{0:T(1024)} %param.29) | copy-start | bytes 24580
  11.8 5.5 %collective-permute-start.2 = (bf16[32,2048]{1,0:T(8,128)(2,1)S(1)}, bf16[32,2048]{1,0:T(8,128)(2,1)S(1)}, u32[]{:S(2)}, u32[]{:S(2)}) collective-permute-start(bf16[32,2048]{1,0:T(8,128)(2,1)S(1)} %get-tuple-element.8), channel_id=1, source_target_pairs={{0,96},{32,0},{64,32},{96,64},{1,97},{33,1},{65,33},{97,65},{2,98}... | collective-permute-start | bytes 393224 | tf_op jit(solution)/shard_map/ppermute | solution.py:41
  15.2 7.2 %collective-permute-start.1 = (bf16[32,2048]{1,0:T(8,128)(2,1)S(1)}, bf16[32,2048]{1,0:T(8,128)(2,1)S(1)}, u32[]{:S(2)}, u32[]{:S(2)}) collective-permute-start(bf16[32,2048]{1,0:T(8,128)(2,1)S(1)} %get-tuple-element.8), channel_id=1, source_target_pairs={{0,32},{32,64},{64,96},{96,0},{1,33},{33,65},{65,97},{97,1},{2,34}... | collective-permute-start | bytes 393224 | tf_op jit(solution)/shard_map/ppermute | solution.py:41
  15.2 7.2 %collective-permute-start = (bf16[32,2048]{1,0:T(8,128)(2,1)S(1)}, bf16[32,2048]{1,0:T(8,128)(2,1)S(1)}, u32[]{:S(2)}, u32[]{:S(2)}) collective-permute-start(bf16[32,2048]{1,0:T(8,128)(2,1)S(1)} %get-tuple-element.8), channel_id=1, source_target_pairs={{0,64},{32,96},{64,0},{96,32},{1,65},{33,97},{65,1},{97,33},{2,66}... | collective-permute-start | bytes 393224 | tf_op jit(solution)/shard_map/ppermute | solution.py:41
  22.6 39.9 %copy-start.3 = (bf16[2,2,352,2048]{3,2,1,0:T(8,128)(2,1)S(1)}, bf16[2,2,352,2048]{3,2,1,0:T(8,128)(2,1)}, u32[]{:S(2)}) copy-start(bf16[2,2,352,2048]{3,2,1,0:T(8,128)(2,1)} %param.32) | copy-start | bytes 17301508
  98.4 9.0 %collective-permute-start.4 = (bf16[32,2048]{1,0:T(8,128)(2,1)S(1)}, bf16[32,2048]{1,0:T(8,128)(2,1)S(1)}, u32[]{:S(2)}, u32[]{:S(2)}) collective-permute-start(bf16[32,2048]{1,0:T(8,128)(2,1)S(1)} %fusion.20), channel_id=1, source_target_pairs={{0,32},{32,64},{64,96},{96,0},{1,33},{33,65},{65,97},{97,1},{2,34}... | collective-permute-start | bytes 393224 | tf_op jit(solution)/shard_map/ppermute | solution.py:41
  98.4 9.0 %collective-permute-start.3 = (bf16[32,2048]{1,0:T(8,128)(2,1)S(1)}, bf16[32,2048]{1,0:T(8,128)(2,1)S(1)}, u32[]{:S(2)}, u32[]{:S(2)}) collective-permute-start(bf16[32,2048]{1,0:T(8,128)(2,1)S(1)} %fusion.20), channel_id=1, source_target_pairs={{0,64},{32,96},{64,0},{96,32},{1,65},{33,97},{65,1},{97,33},{2,66}... | collective-permute-start | bytes 393224 | tf_op jit(solution)/shard_map/ppermute | solution.py:41
  100.1 7.7 %collective-permute-start.5 = (bf16[32,2048]{1,0:T(8,128)(2,1)S(1)}, bf16[32,2048]{1,0:T(8,128)(2,1)S(1)}, u32[]{:S(2)}, u32[]{:S(2)}) collective-permute-start(bf16[32,2048]{1,0:T(8,128)(2,1)S(1)} %fusion.20), channel_id=1, source_target_pairs={{0,96},{32,0},{64,32},{96,64},{1,97},{33,1},{65,33},{97,65},{2,98}... | collective-permute-start | bytes 393224 | tf_op jit(solution)/shard_map/ppermute | solution.py:41

commit v4 on v3

--- a/solution.py
+++ b/solution.py
@@ -8,7 +8,7 @@
 EXPERTS = 64
 MOST = 2
 ROW_Q = 8
-GROUP = 4
+GROUPS = (16, 16)
 
 
 epsilon = 1e-06
@@ -72,9 +72,7 @@
     head_width = nope_width + rope_width
     flat = rows * heads
     score_scale = head_width ** (-0.5)
-    step_rows = GROUP
-    steps = rows // step_rows
-    tile = step_rows * heads
+    starts = [sum(GROUPS[:i]) for i in range(len(GROUPS))]
 
     loads = [
         pltpu.make_async_copy(source, target, load_sems.at[i])
@@ -82,8 +80,8 @@
     ]
     small, early, late = loads[:6], loads[6:10], loads[10:]
     cache = []
-    for i in range(steps):
-        span = pl.ds(i * step_rows, step_rows)
+    for i, (first, size) in enumerate(zip(starts, GROUPS)):
+        span = pl.ds(first, size)
         cache.append(
             (
                 pltpu.make_async_copy(latent_hbm.at[span], latent.at[span], cache_sems.at[i, 0]),
@@ -200,24 +198,27 @@
         + jnp.sum(turned_rows[...].astype(jnp.float32) * key_flat, axis=1, keepdims=True)
     ) * score_scale
 
-    owner = count((tile, 1), 0) // heads
-    places = count((tile, slots), 1).astype(jnp.float32)
-
-    def scores_of(i):
-        span = slice(i * tile, (i + 1) * tile)
+    def scores_of(first, size):
+        tile = size * heads
+        span = slice(first * heads, first * heads + tile)
         query, query_turned = query_rows[span, :], turned_rows[span, :]
+        owner = count((tile, 1), 0) // heads
+        lane_owner = count((1, tile), 1) // heads
         total = jnp.zeros((tile, slots), jnp.float32)
-        for j in range(step_rows):
-            row = i * step_rows + j
+        across = jnp.zeros((slots, tile), jnp.float32)
+        for j in range(size):
             part = lax.dot_general(
-                query, latent[row], (((1,), (1,)), ((), ())), preferred_element_type=jnp.float32
-            ) + jnp.dot(query_turned, rope[row], preferred_element_type=jnp.float32)
+                latent[first + j], query, (((1,), (1,)), ((), ())), preferred_element_type=jnp.float32
+            )
+            across = jnp.where(lane_owner == j, part, across)
+            part = jnp.dot(query_turned, rope[first + j], preferred_element_type=jnp.float32)
             total = jnp.where(owner == j, part, total)
-        return total * score_scale
-
-    def mix(i, scores):
-        span = slice(i * tile, (i + 1) * tile)
-        valid = places < flat_length[span]
+        return (across.T + total) * score_scale
+
+    def mix(first, size, scores):
+        tile = size * heads
+        span = slice(first * heads, first * heads + tile)
+        valid = count((tile, slots), 1).astype(jnp.float32) < flat_length[span]
         own = self_score[span]
         masked = jnp.where(valid, scores, far_below)
         peak = jnp.maximum(jnp.max(masked, axis=1, keepdims=True), own)
@@ -226,21 +227,22 @@
         total = jnp.sum(weights, axis=1, keepdims=True) + self_weight
         probs = (weights / total).astype(jnp.bfloat16)
         prob_self = (self_weight / total).astype(jnp.bfloat16).astype(jnp.float32)
+        owner = count((tile, 1), 0) // heads
         mixed = jnp.zeros((tile, latent_width), jnp.float32)
-        for j in range(step_rows):
-            part = jnp.dot(probs, latent[i * step_rows + j], preferred_element_type=jnp.float32)
+        for j in range(size):
+            part = jnp.dot(probs, latent[first + j], preferred_element_type=jnp.float32)
             mixed = jnp.where(owner == j, part, mixed)
         mixed_rows[span, :] = (mixed + prob_self * latent_flat[span]).astype(jnp.bfloat16)
 
     held = None
-    for i in range(steps):
+    for i, group in enumerate(zip(starts, GROUPS)):
         for copy in cache[i]:
             copy.wait()
-        scores = scores_of(i)
+        scores = scores_of(*group)
         if held is not None:
-            mix(i - 1, held)
-        held = scores
-    mix(steps - 1, held)
+            mix(*held)
+        held = (*group, scores)
+    mix(*held)
 
     for copy in late:
         copy.wait()
@@ -269,7 +271,6 @@
         expert_ids.T, route_weights.T, w_query, w_key_up, w_latent, w_rope_key, w_value_up, w_out,
         latent_cache, rope_cache,
     )
-    steps = rows // GROUP
     return pl.pallas_call(
         attend_kernel,
         out_shape=(
@@ -285,7 +286,7 @@
             pltpu.VMEM((rows * heads, w_rope_key.shape[0]), jnp.bfloat16),
             pltpu.VMEM((rows * heads, latent_width), jnp.bfloat16),
             pltpu.SemaphoreType.DMA((12,)),
-            pltpu.SemaphoreType.DMA((steps, 2)),
+            pltpu.SemaphoreType.DMA((len(GROUPS), 2)),
         ],
         compiler_params=pltpu.CompilerParams(vmem_limit_bytes=40 << 20),
         name="attend_rows",

time: 109 us -> 106 us (0.972)
  Pallas kernels: 11.8 us -> 9.44 us
    pallas_call x1, Pallas kernels: 11.8 us -> 9.44 us  [attend_rows(): pl.pallas_call(attend_kernel, out_shape=(jax.ShapeDtypeStruct((rows, mode...]
where the time goes in v4:
time: 106 us
  blocking collectives  71 us (67%)
  waiting for transfers between devices  12 us (11%)
  Pallas kernels  9.44 us (9%)
  starting transfers between devices  7.85 us (7%)
  matrix products  4.44 us (4%)
    all_to_all x1, blocking collectives, per_device(): lax.all_to_all(packed, 'dev', split_axis=0, concat_axis=0, tiled=True)  39.1 us
    all_to_all x1, blocking collectives, per_device(): lax.all_to_all(partial_out.astype(jnp.bfloat16), 'dev', split_axis=0, con...  31.9 us
    ppermute x6, waiting for transfers between devices, section_sum(): lax.ppermute(partial, 'section', [(i, (i + step) % sections) for i in ran...  12 us
    pallas_call x1, Pallas kernels, attend_rows(): pl.pallas_call(attend_kernel, out_shape=(jax.ShapeDtypeStruct((rows, mode...  9.44 us
    ppermute x6, starting transfers between devices, section_sum(): lax.ppermute(partial, 'section', [(i, (i + step) % sections) for i in ran...  7.85 us
  transfers between devices with their start and end apart: 6, of which 4 were waited for; matrix products, arithmetic and copies ran while one was open for 0% of the time, Pallas kernels for 0%

profile of v4, /device:TPU:1, one launch (start us, length us, event | category | flops | bytes accessed | tf_op | source)
XLA Modules:
  0.0 106.1 jit_solution(5913492794749198786)
XLA Ops:
  0.0 9.4 %attend_rows.1 = (bf16[32,2048]{1,0:T(8,128)(2,1)S(1)}, bf16[32,512]{1,0:T(8,128)(2,1)S(1)}, bf16[64,512]{1,0:T(8,128)(2,1)S(1)}) custom-call(bf16[32,2048]{1,0:T(8,128)(2,1)} %refs_0_.1, s32[1,32]{1,0:T(1,128)} %bitcast.52, f32[1,2048]{1,0:T(1,128)} %bitcast.48, f32[1,512]{1,0:T(1,128)} %bitcast.51, s32[6,32]{1,0:T(8,128)} %bitcast.49, f32[6,32]{1,0:T(8,128)} %bitcast.50, ...), custom_call_target="tpu_custom_call" | custom-call | tf_op jit(solution)/shard_map/attend_rows/pallas_call | solution.py:274
  9.5 3.4 %collective-permute-start.2 = (bf16[32,2048]{1,0:T(8,128)(2,1)S(1)}, bf16[32,2048]{1,0:T(8,128)(2,1)S(1)}, u32[]{:S(2)}, u32[]{:S(2)}) collective-permute-start(bf16[32,2048]{1,0:T(8,128)(2,1)S(1)} %get-tuple-element.8), channel_id=1, source_target_pairs={{0,96},{32,0},{64,32},{96,64},{1,97},{33,1},{65,33},{97,65},{2,98}... | collective-permute-start | bytes 393224 | tf_op jit(solution)/shard_map/ppermute | solution.py:41
  12.8 0.0 collective-permute-start.1
  12.8 1.7 %collective-permute-start = (bf16[32,2048]{1,0:T(8,128)(2,1)S(1)}, bf16[32,2048]{1,0:T(8,128)(2,1)S(1)}, u32[]{:S(2)}, u32[]{:S(2)}) collective-permute-start(bf16[32,2048]{1,0:T(8,128)(2,1)S(1)} %get-tuple-element.8), channel_id=1, source_target_pairs={{0,64},{32,96},{64,0},{96,32},{1,65},{33,97},{65,1},{97,33},{2,66}... | collective-permute-start | bytes 393224 | tf_op jit(solution)/shard_map/ppermute | solution.py:41
  14.6 0.4 collective-permute-done.2
  15.0 5.0 %collective-permute-done.1 = bf16[32,2048]{1,0:T(8,128)(2,1)S(1)} collective-permute-done((bf16[32,2048]{1,0:T(8,128)(2,1)S(1)}, bf16[32,2048]{1,0:T(8,128)(2,1)S(1)}, u32[]{:S(2)}, u32[]{:S(2)}) %collective-permute-start.1) | collective-permute-done | bytes 131104 | tf_op jit(solution)/shard_map/ppermute | solution.py:41
  20.0 0.0 collective-permute-done
  20.0 0.0 copy-done.1
  20.0 0.2 fusion.16
  20.2 0.0 copy-start.3
  20.3 0.8 convolution_convert_fusion
  21.0 39.1 %all_to_all.10 = bf16[32,2,8,2048]{3,2,1,0:T(8,128)(2,1)S(1)} all-to-all(bf16[32,2,8,2048]{3,2,1,0:T(8,128)(2,1)S(1)} %bitcast.47), channel_id=1, replica_groups=mesh['section'=4,'dev'=32] {'dev'}, dimensions={0} | all-to-all | bytes 4194304 | tf_op jit(solution)/shard_map/all_to_all | solution.py:326
  60.1 1.9 %fusion.7 = f32[32,2,8,2,352]{4,2,3,0,1:T(8,128)S(1)} fusion(bf16[2,2,352,2048]{3,2,1,0:T(8,128)(2,1)S(1)} %copy-done.3, bf16[32,2,8,2048]{3,2,1,0:T(8,128)(2,1)S(1)} %all_to_all.10), kind=kOutput, calls=%fused_computation.7 | convolution fusion | flops 1476395008 | bytes 9306112 | tf_op jit(solution)/shard_map/secx,egfx->secgf/dot_general | solution.py:31
  62.0 1.3 %fusion.3 = bf16[32,2,8,2048]{3,2,0,1:T(8,128)(2,1)S(1)} fusion(bf16[2,352,2048]{2,1,0:T(8,128)(2,1)S(1)} %copy-done, f32[32,2,8,2,352]{4,2,3,0,1:T(8,128)S(1)} %fusion.7), kind=kOutput, calls=%fused_computation.5 | convolution fusion | flops 740327424 | bytes 6422528 | tf_op jit(solution)/shard_map/secf,efx->secx/dot_general | solution.py:35
  63.3 0.2 copy.25
  63.6 31.9 %all_to_all.11 = bf16[32,2,8,2048]{3,2,1,0:T(8,128)(2,1)S(1)} all-to-all(bf16[32,2,8,2048]{3,2,1,0:T(8,128)(2,1)S(1)} %copy.25), channel_id=1, replica_groups=mesh['section'=4,'dev'=32] {'dev'}, dimensions={0} | all-to-all | bytes 4194304 | tf_op jit(solution)/shard_map/all_to_all | solution.py:328
  95.5 0.5 fusion.25
  96.0 0.1 collective-permute-start.4
  96.1 1.6 %collective-permute-start.3 = (bf16[32,2048]{1,0:T(8,128)(2,1)S(1)}, bf16[32,2048]{1,0:T(8,128)(2,1)S(1)}, u32[]{:S(2)}, u32[]{:S(2)}) collective-permute-start(bf16[32,2048]{1,0:T(8,128)(2,1)S(1)} %fusion.20), channel_id=1, source_target_pairs={{0,64},{32,96},{64,0},{96,32},{1,65},{33,97},{65,1},{97,33},{2,66}... | collective-permute-start | bytes 393224 | tf_op jit(solution)/shard_map/ppermute | solution.py:41
  97.7 1.1 collective-permute-start.5
  98.7 6.3 %collective-permute-done.4 = bf16[32,2048]{1,0:T(8,128)(2,1)S(1)} collective-permute-done((bf16[32,2048]{1,0:T(8,128)(2,1)S(1)}, bf16[32,2048]{1,0:T(8,128)(2,1)S(1)}, u32[]{:S(2)}, u32[]{:S(2)}) %collective-permute-start.4) | collective-permute-done | bytes 131104 | tf_op jit(solution)/shard_map/ppermute | solution.py:41
  105.0 0.0 collective-permute-done.3
  105.0 0.3 collective-permute-done.5
  105.3 0.8 fusion.19
  (8 shorter events, 0.0 us)
Async XLA Ops:
  0.0 62.0 %copy-start = (bf16[2,352,2048]{2,1,0:T(8,128)(2,1)S(1)}, bf16[2,352,2048]{2,1,0:T(8,128)(2,1)}, u32[]{:S(2)}) copy-start(bf16[2,352,2048]{2,1,0:T(8,128)(2,1)} %param.33) | copy-start | bytes 8650756
  0.0 20.0 %copy-start.1 = (bf16[32,2048]{1,0:T(8,128)(2,1)S(1)}, bf16[32,2048]{1,0:T(8,128)(2,1)}, u32[]{:S(2)}) copy-start(bf16[32,2048]{1,0:T(8,128)(2,1)} %refs_0_.1) | copy-start | bytes 393220
  0.0 20.2 %copy-start.2 = (f32[2048]{0:T(1024)S(1)}, f32[2048]{0:T(1024)}, u32[]{:S(2)}) copy-start(f32[2048]{0:T(1024)} %param.29) | copy-start | bytes 24580
  9.5 5.5 %collective-permute-start.2 = (bf16[32,2048]{1,0:T(8,128)(2,1)S(1)}, bf16[32,2048]{1,0:T(8,128)(2,1)S(1)}, u32[]{:S(2)}, u32[]{:S(2)}) collective-permute-start(bf16[32,2048]{1,0:T(8,128)(2,1)S(1)} %get-tuple-element.8), channel_id=1, source_target_pairs={{0,96},{32,0},{64,32},{96,64},{1,97},{33,1},{65,33},{97,65},{2,98}... | collective-permute-start | bytes 393224 | tf_op jit(solution)/shard_map/ppermute | solution.py:41
  12.8 7.2 %collective-permute-start.1 = (bf16[32,2048]{1,0:T(8,128)(2,1)S(1)}, bf16[32,2048]{1,0:T(8,128)(2,1)S(1)}, u32[]{:S(2)}, u32[]{:S(2)}) collective-permute-start(bf16[32,2048]{1,0:T(8,128)(2,1)S(1)} %get-tuple-element.8), channel_id=1, source_target_pairs={{0,32},{32,64},{64,96},{96,0},{1,33},{33,65},{65,97},{97,1},{2,34}... | collective-permute-start | bytes 393224 | tf_op jit(solution)/shard_map/ppermute | solution.py:41
  12.8 7.2 %collective-permute-start = (bf16[32,2048]{1,0:T(8,128)(2,1)S(1)}, bf16[32,2048]{1,0:T(8,128)(2,1)S(1)}, u32[]{:S(2)}, u32[]{:S(2)}) collective-permute-start(bf16[32,2048]{1,0:T(8,128)(2,1)S(1)} %get-tuple-element.8), channel_id=1, source_target_pairs={{0,64},{32,96},{64,0},{96,32},{1,65},{33,97},{65,1},{97,33},{2,66}... | collective-permute-start | bytes 393224 | tf_op jit(solution)/shard_map/ppermute | solution.py:41
  20.2 39.9 %copy-start.3 = (bf16[2,2,352,2048]{3,2,1,0:T(8,128)(2,1)S(1)}, bf16[2,2,352,2048]{3,2,1,0:T(8,128)(2,1)}, u32[]{:S(2)}) copy-start(bf16[2,2,352,2048]{3,2,1,0:T(8,128)(2,1)} %param.32) | copy-start | bytes 17301508
  96.0 9.0 %collective-permute-start.4 = (bf16[32,2048]{1,0:T(8,128)(2,1)S(1)}, bf16[32,2048]{1,0:T(8,128)(2,1)S(1)}, u32[]{:S(2)}, u32[]{:S(2)}) collective-permute-start(bf16[32,2048]{1,0:T(8,128)(2,1)S(1)} %fusion.20), channel_id=1, source_target_pairs={{0,32},{32,64},{64,96},{96,0},{1,33},{33,65},{65,97},{97,1},{2,34}... | collective-permute-start | bytes 393224 | tf_op jit(solution)/shard_map/ppermute | solution.py:41
  96.1 9.0 %collective-permute-start.3 = (bf16[32,2048]{1,0:T(8,128)(2,1)S(1)}, bf16[32,2048]{1,0:T(8,128)(2,1)S(1)}, u32[]{:S(2)}, u32[]{:S(2)}) collective-permute-start(bf16[32,2048]{1,0:T(8,128)(2,1)S(1)} %fusion.20), channel_id=1, source_target_pairs={{0,64},{32,96},{64,0},{96,32},{1,65},{33,97},{65,1},{97,33},{2,66}... | collective-permute-start | bytes 393224 | tf_op jit(solution)/shard_map/ppermute | solution.py:41
  97.7 7.7 %collective-permute-start.5 = (bf16[32,2048]{1,0:T(8,128)(2,1)S(1)}, bf16[32,2048]{1,0:T(8,128)(2,1)S(1)}, u32[]{:S(2)}, u32[]{:S(2)}) collective-permute-start(bf16[32,2048]{1,0:T(8,128)(2,1)S(1)} %fusion.20), channel_id=1, source_target_pairs={{0,96},{32,0},{64,32},{96,64},{1,97},{33,1},{65,33},{97,65},{2,98}... | collective-permute-start | bytes 393224 | tf_op jit(solution)/shard_map/ppermute | solution.py:41

commit v5 on v4

--- a/solution.py
+++ b/solution.py
@@ -9,6 +9,7 @@
 MOST = 2
 ROW_Q = 8
 GROUPS = (16, 16)
+LANES = 128
 
 
 epsilon = 1e-06
@@ -27,12 +28,31 @@
     return packed.astype(jnp.bfloat16)
 
 
+def expert_kernel(rows_ref, gate_up_ref, down_ref, out_ref):
+    sources, experts, capacity, width = rows_ref.shape
+    contract_last = (((1,), (1,)), ((), ()))
+    for e in range(experts):
+        rows = rows_ref[:, e].reshape(sources * capacity, width)
+        gate = lax.dot_general(
+            rows, gate_up_ref[e, 0], contract_last, preferred_element_type=jnp.float32
+        )
+        up = lax.dot_general(
+            rows, gate_up_ref[e, 1], contract_last, preferred_element_type=jnp.float32
+        )
+        activated = (gate / (1.0 + jnp.exp(-gate)) * up).astype(jnp.bfloat16)
+        out = jnp.dot(activated, down_ref[e], preferred_element_type=jnp.float32)
+        out_ref[:, e] = out.astype(jnp.bfloat16).reshape(sources, capacity, width)
+
+
 def expert_part(slot_rows, w_gate_up, w_down):
-    gate_up = jnp.einsum(
-        "secx,egfx->secgf", slot_rows, w_gate_up, preferred_element_type=jnp.float32
-    )
-    activated = (jax.nn.silu(gate_up[:, :, :, 0, :]) * gate_up[:, :, :, 1, :]).astype(jnp.bfloat16)
-    return jnp.einsum("secf,efx->secx", activated, w_down, preferred_element_type=jnp.float32)
+    return pl.pallas_call(
+        expert_kernel,
+        out_shape=jax.ShapeDtypeStruct(slot_rows.shape, jnp.bfloat16),
+        in_specs=[pl.BlockSpec(memory_space=pltpu.VMEM)] * 3,
+        out_specs=pl.BlockSpec(memory_space=pltpu.VMEM),
+        compiler_params=pltpu.CompilerParams(vmem_limit_bytes=34 << 20),
+        name="expert_part",
+    )(slot_rows, w_gate_up, w_down)
 
 
 def section_sum(partial):
@@ -135,9 +155,6 @@
     flat_length = jnp.sum(repeat * lengths, axis=1, keepdims=True)
     row_length = column(lengths)
     repeat = repeat.astype(jnp.bfloat16)
-    place, other = count((flat, flat), 0), count((flat, flat), 1)
-    order = jnp.where(place == (other % rows) * heads + other // rows, 1.0, 0.0).astype(jnp.bfloat16)
-    back = jnp.where(other == (place % rows) * heads + place // rows, 1.0, 0.0).astype(jnp.bfloat16)
     frequency = jnp.exp(
         -jnp.log(10000.0) * count((1, half), 1).astype(jnp.float32) / half
     )
@@ -157,28 +174,24 @@
     early[0].wait()
     queries = jnp.dot(normed, w_query[...], preferred_element_type=jnp.float32).astype(jnp.bfloat16)
     early[1].wait()
-    by_head, turned_by_head = [], []
+    def wide(ref, span):
+        return jnp.concatenate([ref[c, span, :] for c in range(latent_width // LANES)], axis=1)
+
     for h in range(heads):
         start = h * head_width
-        nope = queries[:, start : start + nope_width]
-        by_head.append(
-            lax.dot_general(
-                nope, w_key_up[h], (((1,), (1,)), ((), ())), preferred_element_type=jnp.float32
-            ).astype(jnp.bfloat16)
+        own_rows = pl.ds(h, rows, stride=heads)
+        middle = start + nope_width
+        in_latent = lax.dot_general(
+            queries[:, start : start + nope_width], w_key_up[h], (((1,), (1,)), ((), ())),
+            preferred_element_type=jnp.float32,
         )
-        middle = start + nope_width
-        turned_by_head.append(
-            turned(
-                queries[:, middle : middle + half].astype(jnp.float32),
-                queries[:, middle + half : middle + rope_width].astype(jnp.float32),
-            )
-        )
-    query_rows[...] = jnp.dot(
-        order, jnp.concatenate(by_head, axis=0), preferred_element_type=jnp.float32
-    ).astype(jnp.bfloat16)
-    turned_rows[...] = jnp.dot(
-        order, jnp.concatenate(turned_by_head, axis=0), preferred_element_type=jnp.float32
-    ).astype(jnp.bfloat16)
+        for c in range(latent_width // LANES):
+            query_rows[c, own_rows, :] = in_latent[:, c * LANES : (c + 1) * LANES]
+        in_rope = turned(
+            queries[:, middle : middle + half].astype(jnp.float32),
+            queries[:, middle + half : middle + rope_width].astype(jnp.float32),
+        ).astype(jnp.float32)
+        turned_rows[own_rows, :] = jnp.concatenate([in_rope, in_rope], axis=1)
 
     early[2].wait()
     latent_raw = jnp.dot(normed, w_latent[...], preferred_element_type=jnp.float32)
@@ -194,26 +207,29 @@
     latent_flat = jnp.dot(repeat, latent_new, preferred_element_type=jnp.float32)
     key_flat = jnp.dot(repeat, key_new, preferred_element_type=jnp.float32)
     self_score = (
-        jnp.sum(query_rows[...].astype(jnp.float32) * latent_flat, axis=1, keepdims=True)
-        + jnp.sum(turned_rows[...].astype(jnp.float32) * key_flat, axis=1, keepdims=True)
+        jnp.sum(wide(query_rows, slice(0, flat)).astype(jnp.bfloat16).astype(jnp.float32) * latent_flat, axis=1, keepdims=True)
+        + jnp.sum(turned_rows[:, 0:rope_width] * key_flat, axis=1, keepdims=True)
     ) * score_scale
 
     def scores_of(first, size):
         tile = size * heads
         span = slice(first * heads, first * heads + tile)
-        query, query_turned = query_rows[span, :], turned_rows[span, :]
+        query = wide(query_rows, span).astype(jnp.bfloat16)
+        query_turned = turned_rows[span, 0:rope_width].astype(jnp.bfloat16)
         owner = count((tile, 1), 0) // heads
         lane_owner = count((1, tile), 1) // heads
         total = jnp.zeros((tile, slots), jnp.float32)
-        across = jnp.zeros((slots, tile), jnp.float32)
+        pieces = []
         for j in range(size):
+            low = j // 4 * 16
             part = lax.dot_general(
-                latent[first + j], query, (((1,), (1,)), ((), ())), preferred_element_type=jnp.float32
-            )
-            across = jnp.where(lane_owner == j, part, across)
-            part = jnp.dot(query_turned, rope[first + j], preferred_element_type=jnp.float32)
-            total = jnp.where(owner == j, part, total)
-        return (across.T + total) * score_scale
+                query[low : low + 16], latent[first + j], (((1,), (1,)), ((), ())),
+                preferred_element_type=jnp.float32,
+            ) + jnp.dot(query_turned[low : low + 16], rope[first + j], preferred_element_type=jnp.float32)
+            near = jnp.where(owner[:16] == j % 4, part, near) if j % 4 else part
+            if j % 4 == 3:
+                pieces.append(near)
+        return jnp.concatenate(pieces, axis=0) * score_scale
 
     def mix(first, size, scores):
         tile = size * heads
@@ -228,11 +244,17 @@
         probs = (weights / total).astype(jnp.bfloat16)
         prob_self = (self_weight / total).astype(jnp.bfloat16).astype(jnp.float32)
         owner = count((tile, 1), 0) // heads
-        mixed = jnp.zeros((tile, latent_width), jnp.float32)
+        pieces = []
         for j in range(size):
-            part = jnp.dot(probs, latent[first + j], preferred_element_type=jnp.float32)
-            mixed = jnp.where(owner == j, part, mixed)
-        mixed_rows[span, :] = (mixed + prob_self * latent_flat[span]).astype(jnp.bfloat16)
+            low = j // 4 * 16
+            part = jnp.dot(probs[low : low + 16], latent[first + j], preferred_element_type=jnp.float32)
+            near = jnp.where(owner[:16] == j % 4, part, near) if j % 4 else part
+            if j % 4 == 3:
+                pieces.append(near)
+        mixed = jnp.concatenate(pieces, axis=0)
+        mixed = mixed + prob_self * latent_flat[span]
+        for c in range(latent_width // LANES):
+            mixed_rows[c, span, :] = mixed[:, c * LANES : (c + 1) * LANES]
 
     held = None
     for i, group in enumerate(zip(starts, GROUPS)):
@@ -246,10 +268,10 @@
 
     for copy in late:
         copy.wait()
-    by_row = jnp.dot(back, mixed_rows[...], preferred_element_type=jnp.float32).astype(jnp.bfloat16)
     outs = [
         jnp.dot(
-            by_row[h * rows : (h + 1) * rows], w_value_up[h], preferred_element_type=jnp.float32
+            wide(mixed_rows, pl.ds(h, rows, stride=heads)).astype(jnp.bfloat16), w_value_up[h],
+            preferred_element_type=jnp.float32,
         ).astype(jnp.bfloat16)
         for h in range(heads)
     ]
@@ -282,9 +304,9 @@
         out_specs=(pl.BlockSpec(memory_space=pltpu.VMEM),) * 3,
         scratch_shapes=[pltpu.VMEM(array.shape, array.dtype) for array in sources]
         + [
-            pltpu.VMEM((rows * heads, latent_width), jnp.bfloat16),
-            pltpu.VMEM((rows * heads, w_rope_key.shape[0]), jnp.bfloat16),
-            pltpu.VMEM((rows * heads, latent_width), jnp.bfloat16),
+            pltpu.VMEM((latent_width // LANES, rows * heads, LANES), jnp.float32),
+            pltpu.VMEM((rows * heads, LANES), jnp.float32),
+            pltpu.VMEM((latent_width // LANES, rows * heads, LANES), jnp.float32),
             pltpu.SemaphoreType.DMA((12,)),
             pltpu.SemaphoreType.DMA((len(GROUPS), 2)),
         ],
@@ -326,7 +348,7 @@
         lax.all_to_all(packed, "dev", split_axis=0, concat_axis=0, tiled=True), w_gate_up, w_down
     )
     returned = lax.all_to_all(
-        partial_out.astype(jnp.bfloat16), "dev", split_axis=0, concat_axis=0, tiled=True
+        partial_out, "dev", split_axis=0, concat_axis=0, tiled=True
     )
     routed = section_sum(combine_rows(returned, mix).astype(jnp.bfloat16))
     return (middle.astype(jnp.float32) + routed).astype(jnp.bfloat16)

time: 106 us -> 106 us (level)
  Pallas kernels: 9.44 us -> 12.8 us
  matrix products: 4.44 us -> 1.23 us
    pallas_call x0 -> x1, Pallas kernels: none -> 3.58 us  [expert_part(): pl.pallas_call(expert_kernel, out_shape=jax.ShapeDtypeStruct(slot_rows.sh...]
    dot_general x2 -> x0, matrix products: 3.21 us -> none  [the longest x1 1.92 us: expert_part(): jnp.einsum('secx,egfx->secgf', slot_rows, w_gate_up, preferred_element_ty...]
where the time goes in v5:
time: 106 us
  blocking collectives  71 us (67%)
  Pallas kernels  12.8 us (12%)
  waiting for transfers between devices  12 us (11%)
  starting transfers between devices  7.85 us (7%)
  matrix products  1.23 us (1%)
    all_to_all x1, blocking collectives, per_device(): lax.all_to_all(packed, 'dev', split_axis=0, concat_axis=0, tiled=True)  39.1 us
    all_to_all x1, blocking collectives, per_device(): lax.all_to_all(partial_out, 'dev', split_axis=0, concat_axis=0, tiled=True)  31.9 us
    ppermute x6, waiting for transfers between devices, section_sum(): lax.ppermute(partial, 'section', [(i, (i + step) % sections) for i in ran...  12 us
    pallas_call x1, Pallas kernels, attend_rows(): pl.pallas_call(attend_kernel, out_shape=(jax.ShapeDtypeStruct((rows, mode...  9.21 us
    ppermute x6, starting transfers between devices, section_sum(): lax.ppermute(partial, 'section', [(i, (i + step) % sections) for i in ran...  7.85 us
    pallas_call x1, Pallas kernels, expert_part(): pl.pallas_call(expert_kernel, out_shape=jax.ShapeDtypeStruct(slot_rows.sh...  3.58 us
  transfers between devices with their start and end apart: 6, of which 4 were waited for; matrix products, arithmetic and copies ran while one was open for 0% of the time, Pallas kernels for 0%

profile of v5, /device:TPU:1, one launch (start us, length us, event | category | flops | bytes accessed | tf_op | source)
XLA Modules:
  0.0 106.0 jit_solution(17977127792844917390)
XLA Ops:
  0.0 9.2 %attend_rows.1 = (bf16[32,2048]{1,0:T(8,128)(2,1)S(1)}, bf16[32,512]{1,0:T(8,128)(2,1)S(1)}, bf16[64,512]{1,0:T(8,128)(2,1)S(1)}) custom-call(bf16[32,2048]{1,0:T(8,128)(2,1)} %refs_0_.1, s32[1,32]{1,0:T(1,128)} %bitcast.16, f32[1,2048]{1,0:T(1,128)} %bitcast.12, f32[1,512]{1,0:T(1,128)} %bitcast.15, s32[6,32]{1,0:T(8,128)} %bitcast.13, f32[6,32]{1,0:T(8,128)} %bitcast.14, ...), custom_call_target="tpu_custom_call" | custom-call | tf_op jit(solution)/shard_map/attend_rows/pallas_call | solution.py:296
  9.2 3.4 %collective-permute-start.2 = (bf16[32,2048]{1,0:T(8,128)(2,1)S(1)}, bf16[32,2048]{1,0:T(8,128)(2,1)S(1)}, u32[]{:S(2)}, u32[]{:S(2)}) collective-permute-start(bf16[32,2048]{1,0:T(8,128)(2,1)S(1)} %get-tuple-element.8), channel_id=1, source_target_pairs={{0,96},{32,0},{64,32},{96,64},{1,97},{33,1},{65,33},{97,65},{2,98}... | collective-permute-start | bytes 393224 | tf_op jit(solution)/shard_map/ppermute | solution.py:61
  12.6 0.0 collective-permute-start.1
  12.6 1.7 %collective-permute-start = (bf16[32,2048]{1,0:T(8,128)(2,1)S(1)}, bf16[32,2048]{1,0:T(8,128)(2,1)S(1)}, u32[]{:S(2)}, u32[]{:S(2)}) collective-permute-start(bf16[32,2048]{1,0:T(8,128)(2,1)S(1)} %get-tuple-element.8), channel_id=1, source_target_pairs={{0,64},{32,96},{64,0},{96,32},{1,65},{33,97},{65,1},{97,33},{2,66}... | collective-permute-start | bytes 393224 | tf_op jit(solution)/shard_map/ppermute | solution.py:61
  14.3 0.4 collective-permute-done.2
  14.8 5.0 %collective-permute-done.1 = bf16[32,2048]{1,0:T(8,128)(2,1)S(1)} collective-permute-done((bf16[32,2048]{1,0:T(8,128)(2,1)S(1)}, bf16[32,2048]{1,0:T(8,128)(2,1)S(1)}, u32[]{:S(2)}, u32[]{:S(2)}) %collective-permute-start.1) | collective-permute-done | bytes 131104 | tf_op jit(solution)/shard_map/ppermute | solution.py:61
  19.8 0.0 collective-permute-done
  19.8 0.0 copy-done.2
  19.8 0.2 fusion
  20.0 0.0 copy-done.3
  20.0 0.0 copy-start
  20.0 0.8 convolution_convert_fusion
  20.8 39.1 %all_to_all.10.rows_ref = bf16[32,2,8,2048]{3,2,1,0:T(8,128)(2,1)S(1)} all-to-all(bf16[32,2,8,2048]{3,2,1,0:T(8,128)(2,1)S(1)} %bitcast.11), channel_id=1, replica_groups=mesh['section'=4,'dev'=32] {'dev'}, dimensions={0} | all-to-all | bytes 4194304 | tf_op jit(solution)/shard_map/all_to_all | solution.py:348
  59.9 0.0 copy-done
  59.9 3.6 %expert_part.1 = bf16[32,2,8,2048]{3,2,1,0:T(8,128)(2,1)S(1)} custom-call(bf16[32,2,8,2048]{3,2,1,0:T(8,128)(2,1)S(1)} %all_to_all.10.rows_ref, bf16[2,2,352,2048]{3,2,1,0:T(8,128)(2,1)S(1)} %copy-done, bf16[2,352,2048]{2,1,0:T(8,128)(2,1)S(1)} %copy-done.1), custom_call_target="tpu_custom_call" | custom-call | tf_op jit(solution)/shard_map/expert_part/pallas_call | solution.py:48
  63.4 31.9 %all_to_all.11 = bf16[32,2,8,2048]{3,2,1,0:T(8,128)(2,1)S(1)} all-to-all(bf16[32,2,8,2048]{3,2,1,0:T(8,128)(2,1)S(1)} %expert_part.1), channel_id=1, replica_groups=mesh['section'=4,'dev'=32] {'dev'}, dimensions={0} | all-to-all | bytes 4194304 | tf_op jit(solution)/shard_map/all_to_all | solution.py:350
  95.3 0.5 fusion.8
  95.9 0.1 collective-permute-start.4
  95.9 1.6 %collective-permute-start.3 = (bf16[32,2048]{1,0:T(8,128)(2,1)S(1)}, bf16[32,2048]{1,0:T(8,128)(2,1)S(1)}, u32[]{:S(2)}, u32[]{:S(2)}) collective-permute-start(bf16[32,2048]{1,0:T(8,128)(2,1)S(1)} %fusion.4), channel_id=1, source_target_pairs={{0,64},{32,96},{64,0},{96,32},{1,65},{33,97},{65,1},{97,33},{2,66}... | collective-permute-start | bytes 393224 | tf_op jit(solution)/shard_map/ppermute | solution.py:61
  97.6 1.1 collective-permute-start.5
  98.6 6.3 %collective-permute-done.4 = bf16[32,2048]{1,0:T(8,128)(2,1)S(1)} collective-permute-done((bf16[32,2048]{1,0:T(8,128)(2,1)S(1)}, bf16[32,2048]{1,0:T(8,128)(2,1)S(1)}, u32[]{:S(2)}, u32[]{:S(2)}) %collective-permute-start.4) | collective-permute-done | bytes 131104 | tf_op jit(solution)/shard_map/ppermute | solution.py:61
  104.9 0.0 collective-permute-done.3
  104.9 0.3 collective-permute-done.5
  105.2 0.8 fusion.3
  (6 shorter events, 0.0 us)
Async XLA Ops:
  0.0 19.8 %copy-start.2 = (bf16[32,2048]{1,0:T(8,128)(2,1)S(1)}, bf16[32,2048]{1,0:T(8,128)(2,1)}, u32[]{:S(2)}) copy-start(bf16[32,2048]{1,0:T(8,128)(2,1)} %refs_0_.1) | copy-start | bytes 393220
  0.0 20.0 %copy-start.3 = (f32[2048]{0:T(1024)S(1)}, f32[2048]{0:T(1024)}, u32[]{:S(2)}) copy-start(f32[2048]{0:T(1024)} %param.29) | copy-start | bytes 24580
  0.0 59.8 %copy-start.1 = (bf16[2,352,2048]{2,1,0:T(8,128)(2,1)S(1)}, bf16[2,352,2048]{2,1,0:T(8,128)(2,1)}, u32[]{:S(2)}) copy-start(bf16[2,352,2048]{2,1,0:T(8,128)(2,1)} %down_ref.1) | copy-start | bytes 8650756
  9.2 5.5 %collective-permute-start.2 = (bf16[32,2048]{1,0:T(8,128)(2,1)S(1)}, bf16[32,2048]{1,0:T(8,128)(2,1)S(1)}, u32[]{:S(2)}, u32[]{:S(2)}) collective-permute-start(bf16[32,2048]{1,0:T(8,128)(2,1)S(1)} %get-tuple-element.8), channel_id=1, source_target_pairs={{0,96},{32,0},{64,32},{96,64},{1,97},{33,1},{65,33},{97,65},{2,98}... | collective-permute-start | bytes 393224 | tf_op jit(solution)/shard_map/ppermute | solution.py:61
  12.6 7.2 %collective-permute-start.1 = (bf16[32,2048]{1,0:T(8,128)(2,1)S(1)}, bf16[32,2048]{1,0:T(8,128)(2,1)S(1)}, u32[]{:S(2)}, u32[]{:S(2)}) collective-permute-start(bf16[32,2048]{1,0:T(8,128)(2,1)S(1)} %get-tuple-element.8), channel_id=1, source_target_pairs={{0,32},{32,64},{64,96},{96,0},{1,33},{33,65},{65,97},{97,1},{2,34}... | collective-permute-start | bytes 393224 | tf_op jit(solution)/shard_map/ppermute | solution.py:61
  12.6 7.2 %collective-permute-start = (bf16[32,2048]{1,0:T(8,128)(2,1)S(1)}, bf16[32,2048]{1,0:T(8,128)(2,1)S(1)}, u32[]{:S(2)}, u32[]{:S(2)}) collective-permute-start(bf16[32,2048]{1,0:T(8,128)(2,1)S(1)} %get-tuple-element.8), channel_id=1, source_target_pairs={{0,64},{32,96},{64,0},{96,32},{1,65},{33,97},{65,1},{97,33},{2,66}... | collective-permute-start | bytes 393224 | tf_op jit(solution)/shard_map/ppermute | solution.py:61
  20.0 39.8 %copy-start = (bf16[2,2,352,2048]{3,2,1,0:T(8,128)(2,1)S(1)}, bf16[2,2,352,2048]{3,2,1,0:T(8,128)(2,1)}, u32[]{:S(2)}) copy-start(bf16[2,2,352,2048]{3,2,1,0:T(8,128)(2,1)} %gate_up_ref.1) | copy-start | bytes 17301508
  95.9 9.0 %collective-permute-start.4 = (bf16[32,2048]{1,0:T(8,128)(2,1)S(1)}, bf16[32,2048]{1,0:T(8,128)(2,1)S(1)}, u32[]{:S(2)}, u32[]{:S(2)}) collective-permute-start(bf16[32,2048]{1,0:T(8,128)(2,1)S(1)} %fusion.4), channel_id=1, source_target_pairs={{0,32},{32,64},{64,96},{96,0},{1,33},{33,65},{65,97},{97,1},{2,34}... | collective-permute-start | bytes 393224 | tf_op jit(solution)/shard_map/ppermute | solution.py:61
  95.9 9.0 %collective-permute-start.3 = (bf16[32,2048]{1,0:T(8,128)(2,1)S(1)}, bf16[32,2048]{1,0:T(8,128)(2,1)S(1)}, u32[]{:S(2)}, u32[]{:S(2)}) collective-permute-start(bf16[32,2048]{1,0:T(8,128)(2,1)S(1)} %fusion.4), channel_id=1, source_target_pairs={{0,64},{32,96},{64,0},{96,32},{1,65},{33,97},{65,1},{97,33},{2,66}... | collective-permute-start | bytes 393224 | tf_op jit(solution)/shard_map/ppermute | solution.py:61
  97.6 7.7 %collective-permute-start.5 = (bf16[32,2048]{1,0:T(8,128)(2,1)S(1)}, bf16[32,2048]{1,0:T(8,128)(2,1)S(1)}, u32[]{:S(2)}, u32[]{:S(2)}) collective-permute-start(bf16[32,2048]{1,0:T(8,128)(2,1)S(1)} %fusion.4), channel_id=1, source_target_pairs={{0,96},{32,0},{64,32},{96,64},{1,97},{33,1},{65,33},{97,65},{2,98}... | collective-permute-start | bytes 393224 | tf_op jit(solution)/shard_map/ppermute | solution.py:61

commit v6 on v5

--- a/solution.py
+++ b/solution.py
@@ -31,17 +31,22 @@
 def expert_kernel(rows_ref, gate_up_ref, down_ref, out_ref):
     sources, experts, capacity, width = rows_ref.shape
     contract_last = (((1,), (1,)), ((), ()))
+    activated = []
     for e in range(experts):
         rows = rows_ref[:, e].reshape(sources * capacity, width)
         gate = lax.dot_general(
-            rows, gate_up_ref[e, 0], contract_last, preferred_element_type=jnp.float32
+            gate_up_ref[e, 0], rows, contract_last, preferred_element_type=jnp.float32
         )
         up = lax.dot_general(
-            rows, gate_up_ref[e, 1], contract_last, preferred_element_type=jnp.float32
+            gate_up_ref[e, 1], rows, contract_last, preferred_element_type=jnp.float32
         )
-        activated = (gate / (1.0 + jnp.exp(-gate)) * up).astype(jnp.bfloat16)
-        out = jnp.dot(activated, down_ref[e], preferred_element_type=jnp.float32)
-        out_ref[:, e] = out.astype(jnp.bfloat16).reshape(sources, capacity, width)
+        activated.append((gate / (1.0 + jnp.exp(-gate)) * up).astype(jnp.bfloat16).T)
+    half = width // 2
+    for e in range(experts):
+        for start in (0, half):
+            span = slice(start, start + half)
+            out = jnp.dot(activated[e], down_ref[e, :, span], preferred_element_type=jnp.float32)
+            out_ref[:, e, :, span] = out.astype(jnp.bfloat16).reshape(sources, capacity, half)
 
 
 def expert_part(slot_rows, w_gate_up, w_down):

time: 106 us -> 105 us (level)
  no operation moved by 1% of the time
where the time goes in v6:
time: 105 us
  blocking collectives  71 us (68%)
  Pallas kernels  12 us (11%)
  waiting for transfers between devices  12 us (11%)
  starting transfers between devices  7.85 us (7%)
  matrix products  1.24 us (1%)
    all_to_all x1, blocking collectives, per_device(): lax.all_to_all(packed, 'dev', split_axis=0, concat_axis=0, tiled=True)  39.1 us
    all_to_all x1, blocking collectives, per_device(): lax.all_to_all(partial_out, 'dev', split_axis=0, concat_axis=0, tiled=True)  31.9 us
    ppermute x6, waiting for transfers between devices, section_sum(): lax.ppermute(partial, 'section', [(i, (i + step) % sections) for i in ran...  12 us
    pallas_call x1, Pallas kernels, attend_rows(): pl.pallas_call(attend_kernel, out_shape=(jax.ShapeDtypeStruct((rows, mode...  9.21 us
    ppermute x6, starting transfers between devices, section_sum(): lax.ppermute(partial, 'section', [(i, (i + step) % sections) for i in ran...  7.85 us
    pallas_call x1, Pallas kernels, expert_part(): pl.pallas_call(expert_kernel, out_shape=jax.ShapeDtypeStruct(slot_rows.sh...  2.8 us
  transfers between devices with their start and end apart: 6, of which 4 were waited for; matrix products, arithmetic and copies ran while one was open for 0% of the time, Pallas kernels for 0%

profile of v6, /device:TPU:1, one launch (start us, length us, event | category | flops | bytes accessed | tf_op | source)
XLA Modules:
  0.0 105.2 jit_solution(16256172427660433031)
XLA Ops:
  0.0 9.2 %attend_rows.1 = (bf16[32,2048]{1,0:T(8,128)(2,1)S(1)}, bf16[32,512]{1,0:T(8,128)(2,1)S(1)}, bf16[64,512]{1,0:T(8,128)(2,1)S(1)}) custom-call(bf16[32,2048]{1,0:T(8,128)(2,1)} %refs_0_.1, s32[1,32]{1,0:T(1,128)} %bitcast.16, f32[1,2048]{1,0:T(1,128)} %bitcast.12, f32[1,512]{1,0:T(1,128)} %bitcast.15, s32[6,32]{1,0:T(8,128)} %bitcast.13, f32[6,32]{1,0:T(8,128)} %bitcast.14, ...), custom_call_target="tpu_custom_call" | custom-call | tf_op jit(solution)/shard_map/attend_rows/pallas_call | solution.py:301
  9.2 3.4 %collective-permute-start.2 = (bf16[32,2048]{1,0:T(8,128)(2,1)S(1)}, bf16[32,2048]{1,0:T(8,128)(2,1)S(1)}, u32[]{:S(2)}, u32[]{:S(2)}) collective-permute-start(bf16[32,2048]{1,0:T(8,128)(2,1)S(1)} %get-tuple-element.8), channel_id=1, source_target_pairs={{0,96},{32,0},{64,32},{96,64},{1,97},{33,1},{65,33},{97,65},{2,98}... | collective-permute-start | bytes 393224 | tf_op jit(solution)/shard_map/ppermute | solution.py:66
  12.6 0.0 collective-permute-start.1
  12.6 1.7 %collective-permute-start = (bf16[32,2048]{1,0:T(8,128)(2,1)S(1)}, bf16[32,2048]{1,0:T(8,128)(2,1)S(1)}, u32[]{:S(2)}, u32[]{:S(2)}) collective-permute-start(bf16[32,2048]{1,0:T(8,128)(2,1)S(1)} %get-tuple-element.8), channel_id=1, source_target_pairs={{0,64},{32,96},{64,0},{96,32},{1,65},{33,97},{65,1},{97,33},{2,66}... | collective-permute-start | bytes 393224 | tf_op jit(solution)/shard_map/ppermute | solution.py:66
  14.3 0.4 collective-permute-done.2
  14.8 5.0 %collective-permute-done.1 = bf16[32,2048]{1,0:T(8,128)(2,1)S(1)} collective-permute-done((bf16[32,2048]{1,0:T(8,128)(2,1)S(1)}, bf16[32,2048]{1,0:T(8,128)(2,1)S(1)}, u32[]{:S(2)}, u32[]{:S(2)}) %collective-permute-start.1) | collective-permute-done | bytes 131104 | tf_op jit(solution)/shard_map/ppermute | solution.py:66
  19.8 0.0 collective-permute-done
  19.8 0.0 copy-done.2
  19.8 0.2 fusion
  20.0 0.0 copy-done.3
  20.0 0.0 copy-start
  20.0 0.8 convolution_convert_fusion
  20.8 39.1 %all_to_all.10.rows_ref = bf16[32,2,8,2048]{3,2,1,0:T(8,128)(2,1)S(1)} all-to-all(bf16[32,2,8,2048]{3,2,1,0:T(8,128)(2,1)S(1)} %bitcast.11), channel_id=1, replica_groups=mesh['section'=4,'dev'=32] {'dev'}, dimensions={0} | all-to-all | bytes 4194304 | tf_op jit(solution)/shard_map/all_to_all | solution.py:353
  59.9 0.0 copy-done
  59.9 2.8 %expert_part.1 = bf16[32,2,8,2048]{3,2,1,0:T(8,128)(2,1)S(1)} custom-call(bf16[32,2,8,2048]{3,2,1,0:T(8,128)(2,1)S(1)} %all_to_all.10.rows_ref, bf16[2,2,352,2048]{3,2,1,0:T(8,128)(2,1)S(1)} %copy-done, bf16[2,352,2048]{2,1,0:T(8,128)(2,1)S(1)} %copy-done.1), custom_call_target="tpu_custom_call" | custom-call | tf_op jit(solution)/shard_map/expert_part/pallas_call | solution.py:53
  62.7 31.9 %all_to_all.11 = bf16[32,2,8,2048]{3,2,1,0:T(8,128)(2,1)S(1)} all-to-all(bf16[32,2,8,2048]{3,2,1,0:T(8,128)(2,1)S(1)} %expert_part.1), channel_id=1, replica_groups=mesh['section'=4,'dev'=32] {'dev'}, dimensions={0} | all-to-all | bytes 4194304 | tf_op jit(solution)/shard_map/all_to_all | solution.py:355
  94.6 0.5 fusion.8
  95.1 0.1 collective-permute-start.4
  95.2 1.6 %collective-permute-start.3 = (bf16[32,2048]{1,0:T(8,128)(2,1)S(1)}, bf16[32,2048]{1,0:T(8,128)(2,1)S(1)}, u32[]{:S(2)}, u32[]{:S(2)}) collective-permute-start(bf16[32,2048]{1,0:T(8,128)(2,1)S(1)} %fusion.4), channel_id=1, source_target_pairs={{0,64},{32,96},{64,0},{96,32},{1,65},{33,97},{65,1},{97,33},{2,66}... | collective-permute-start | bytes 393224 | tf_op jit(solution)/shard_map/ppermute | solution.py:66
  96.8 1.0 collective-permute-start.5
  97.8 6.3 %collective-permute-done.4 = bf16[32,2048]{1,0:T(8,128)(2,1)S(1)} collective-permute-done((bf16[32,2048]{1,0:T(8,128)(2,1)S(1)}, bf16[32,2048]{1,0:T(8,128)(2,1)S(1)}, u32[]{:S(2)}, u32[]{:S(2)}) %collective-permute-start.4) | collective-permute-done | bytes 131104 | tf_op jit(solution)/shard_map/ppermute | solution.py:66
  104.1 0.0 collective-permute-done.3
  104.1 0.3 collective-permute-done.5
  104.4 0.8 fusion.3
  (6 shorter events, 0.0 us)
Async XLA Ops:
  0.0 19.8 %copy-start.2 = (bf16[32,2048]{1,0:T(8,128)(2,1)S(1)}, bf16[32,2048]{1,0:T(8,128)(2,1)}, u32[]{:S(2)}) copy-start(bf16[32,2048]{1,0:T(8,128)(2,1)} %refs_0_.1) | copy-start | bytes 393220
  0.0 20.0 %copy-start.3 = (f32[2048]{0:T(1024)S(1)}, f32[2048]{0:T(1024)}, u32[]{:S(2)}) copy-start(f32[2048]{0:T(1024)} %param.29) | copy-start | bytes 24580
  0.0 59.8 %copy-start.1 = (bf16[2,352,2048]{2,1,0:T(8,128)(2,1)S(1)}, bf16[2,352,2048]{2,1,0:T(8,128)(2,1)}, u32[]{:S(2)}) copy-start(bf16[2,352,2048]{2,1,0:T(8,128)(2,1)} %down_ref.1) | copy-start | bytes 8650756
  9.2 5.5 %collective-permute-start.2 = (bf16[32,2048]{1,0:T(8,128)(2,1)S(1)}, bf16[32,2048]{1,0:T(8,128)(2,1)S(1)}, u32[]{:S(2)}, u32[]{:S(2)}) collective-permute-start(bf16[32,2048]{1,0:T(8,128)(2,1)S(1)} %get-tuple-element.8), channel_id=1, source_target_pairs={{0,96},{32,0},{64,32},{96,64},{1,97},{33,1},{65,33},{97,65},{2,98}... | collective-permute-start | bytes 393224 | tf_op jit(solution)/shard_map/ppermute | solution.py:66
  12.6 7.2 %collective-permute-start.1 = (bf16[32,2048]{1,0:T(8,128)(2,1)S(1)}, bf16[32,2048]{1,0:T(8,128)(2,1)S(1)}, u32[]{:S(2)}, u32[]{:S(2)}) collective-permute-start(bf16[32,2048]{1,0:T(8,128)(2,1)S(1)} %get-tuple-element.8), channel_id=1, source_target_pairs={{0,32},{32,64},{64,96},{96,0},{1,33},{33,65},{65,97},{97,1},{2,34}... | collective-permute-start | bytes 393224 | tf_op jit(solution)/shard_map/ppermute | solution.py:66
  12.6 7.2 %collective-permute-start = (bf16[32,2048]{1,0:T(8,128)(2,1)S(1)}, bf16[32,2048]{1,0:T(8,128)(2,1)S(1)}, u32[]{:S(2)}, u32[]{:S(2)}) collective-permute-start(bf16[32,2048]{1,0:T(8,128)(2,1)S(1)} %get-tuple-element.8), channel_id=1, source_target_pairs={{0,64},{32,96},{64,0},{96,32},{1,65},{33,97},{65,1},{97,33},{2,66}... | collective-permute-start | bytes 393224 | tf_op jit(solution)/shard_map/ppermute | solution.py:66
  20.0 39.8 %copy-start = (bf16[2,2,352,2048]{3,2,1,0:T(8,128)(2,1)S(1)}, bf16[2,2,352,2048]{3,2,1,0:T(8,128)(2,1)}, u32[]{:S(2)}) copy-start(bf16[2,2,352,2048]{3,2,1,0:T(8,128)(2,1)} %gate_up_ref.1) | copy-start | bytes 17301508
  95.1 9.0 %collective-permute-start.4 = (bf16[32,2048]{1,0:T(8,128)(2,1)S(1)}, bf16[32,2048]{1,0:T(8,128)(2,1)S(1)}, u32[]{:S(2)}, u32[]{:S(2)}) collective-permute-start(bf16[32,2048]{1,0:T(8,128)(2,1)S(1)} %fusion.4), channel_id=1, source_target_pairs={{0,32},{32,64},{64,96},{96,0},{1,33},{33,65},{65,97},{97,1},{2,34}... | collective-permute-start | bytes 393224 | tf_op jit(solution)/shard_map/ppermute | solution.py:66
  95.2 9.0 %collective-permute-start.3 = (bf16[32,2048]{1,0:T(8,128)(2,1)S(1)}, bf16[32,2048]{1,0:T(8,128)(2,1)S(1)}, u32[]{:S(2)}, u32[]{:S(2)}) collective-permute-start(bf16[32,2048]{1,0:T(8,128)(2,1)S(1)} %fusion.4), channel_id=1, source_target_pairs={{0,64},{32,96},{64,0},{96,32},{1,65},{33,97},{65,1},{97,33},{2,66}... | collective-permute-start | bytes 393224 | tf_op jit(solution)/shard_map/ppermute | solution.py:66
  96.8 7.6 %collective-permute-start.5 = (bf16[32,2048]{1,0:T(8,128)(2,1)S(1)}, bf16[32,2048]{1,0:T(8,128)(2,1)S(1)}, u32[]{:S(2)}, u32[]{:S(2)}) collective-permute-start(bf16[32,2048]{1,0:T(8,128)(2,1)S(1)} %fusion.4), channel_id=1, source_target_pairs={{0,96},{32,0},{64,32},{96,64},{1,97},{33,1},{65,33},{97,65},{2,98}... | collective-permute-start | bytes 393224 | tf_op jit(solution)/shard_map/ppermute | solution.py:66
